TPU v7x, 256 devices: a whole 4x4x8 slice. The times are simulated.
256 devices in a mesh: src: 16 (over y_lo, x, core), tgt: 16 (over z, y_hi).
Axes of the slice: x: 4, y: 4 (y_hi: 2, y_lo: 2; y = y_hi * 2 + y_lo), z: 8, core: 2. Of those that a mesh axis runs over, the one named last changes fastest.
Arguments:
- feature_a: bfloat16 [16, 128, 1024], P('src', 'tgt'), may hold values from -6 to 6
- feature_b: bfloat16 [32, 32, 1024], P('tgt', 'src'), may hold values from -6 to 6
- conv_in: float32 [8, 81], replicated, may hold values from -0.625 to 0.625
- bias_in: float32 [8], replicated, may hold values from -4 to 4
- conv_out: float32 [8, 81], replicated, may hold values from -0.25 to 0.25
Outputs:
- consensus: float32 [32, 32, 16, 128], P('tgt', 'src')
All inputs are finite; a program needn't handle non-finite values.
Results may differ from a plain program's by a relative error of at most 0.0024.
Values may be sent and summed in bfloat16 or wider, within the bound.
No kernel may reach another device: no remote copies, remote signals or barrier semaphores. Data moves between devices by JAX's collectives and lax.ppermute only.
A program may use at most 64 MiB of HBM per device.

v0:
```python
import jax
import jax.numpy as jnp
from jax import lax
from jax.sharding import PartitionSpec as P


def extended_2(block, sides, width):
    for axis, dim in sides:
        count = lax.axis_size(axis)
        forward = [(i, i + 1) for i in range(count - 1)]
        backward = [(target, source) for source, target in forward]
        low = lax.ppermute(
            lax.slice_in_dim(block, block.shape[dim] - width, None, axis=dim), axis, forward
        )
        high = lax.ppermute(lax.slice_in_dim(block, 0, width, axis=dim), axis, backward)
        block = jnp.concatenate([low, block, high], axis=dim)
    return block


def filter_taps(source, weights, extent):
    summed_total = jnp.zeros(extent, jnp.float32)
    for first in range(3):
        for second in range(3):
            for third in range(3):
                for fourth in range(3):
                    weight = weights[first * 27 + second * 9 + third * 3 + fourth]
                    summed_total = (
                        summed_total
                        + weight
                        * source[
                            first : first + extent[0],
                            second : second + extent[1],
                            third : third + extent[2],
                            fourth : fourth + extent[3],
                        ]
                    )
    return summed_total


def per_device(feature_a, feature_b, conv_in, bias_in, conv_out):
    rows_b = feature_b.shape[0]
    cols_b = feature_b.shape[1]
    channels = feature_b.shape[2]
    ext_r = feature_b.shape[0]
    ext_c = feature_b.shape[1]
    flat_b = feature_b.reshape(ext_r * ext_c, channels)
    wide = lax.all_gather(feature_a, "tgt", axis=1, tiled=True)
    piece = lax.all_gather(wide, "src", axis=0, tiled=True)
    count_r = piece.shape[0]
    count_c = piece.shape[1]
    scores = jnp.einsum(
        "qc,pc->qp",
        flat_b,
        piece.reshape(count_r * count_c, channels),
        preferred_element_type=jnp.float32,
    )
    scores = (scores * channels ** (-0.5)).astype(jnp.bfloat16)
    volume = scores.reshape(ext_r, ext_c, count_r, count_c)
    volume = extended_2(volume, (("src", 1), ("tgt", 0)), 2)
    source_rows = volume.shape[2]
    source_cols = volume.shape[3]
    border_padding = ((0, 0), (0, 0), (1, 1), (1, 1))
    field = jnp.pad(volume.astype(jnp.float32), border_padding)
    total_r = rows_b * lax.axis_size("tgt")
    total_c = cols_b * lax.axis_size("src")
    index_r = lax.axis_index("tgt") * rows_b - 1 + jnp.arange(rows_b + 2, dtype=jnp.int32)
    index_c = lax.axis_index("src") * cols_b - 1 + jnp.arange(cols_b + 2, dtype=jnp.int32)
    inside_r = ((index_r >= 0) & (index_r < total_r)).astype(jnp.float32)
    inside_c = ((index_c >= 0) & (index_c < total_c)).astype(jnp.float32)
    inside = inside_r[:, None, None, None] * inside_c[None, :, None, None]
    hidden_count = conv_in.shape[0]
    mirror_in = (
        conv_in.reshape(hidden_count, 3, 3, 3, 3).transpose(0, 3, 4, 1, 2).reshape(hidden_count, 81)
    )
    reflected_output = (
        conv_out.reshape(hidden_count, 3, 3, 3, 3)
        .transpose(0, 3, 4, 1, 2)
        .reshape(hidden_count, 81)
    )
    extended = (rows_b + 2, cols_b + 2, source_rows, source_cols)
    local_entries = (rows_b, cols_b, source_rows, source_cols)

    def channel_step(channel_slot, summed_total):
        hidden_fwd = (
            jax.nn.relu(filter_taps(field, conv_in[channel_slot], extended) + bias_in[channel_slot])
            * inside
        )
        hidden_reflected = (
            jax.nn.relu(
                filter_taps(field, mirror_in[channel_slot], extended) + bias_in[channel_slot]
            )
            * inside
        )
        summed_total = summed_total + filter_taps(
            jnp.pad(hidden_fwd, border_padding), conv_out[channel_slot], local_entries
        )
        return summed_total + filter_taps(
            jnp.pad(hidden_reflected, border_padding), reflected_output[channel_slot], local_entries
        )

    return lax.fori_loop(0, hidden_count, channel_step, jnp.zeros(local_entries, jnp.float32))


def solution(mesh):
    in_specs = (P("src", "tgt", None), P("tgt", "src", None), P(), P(), P())
    out_specs = P("tgt", "src", None, None)
    return jax.shard_map(
        per_device, mesh=mesh, in_specs=in_specs, out_specs=out_specs, check_vma=False
    )
```

profile of v0, /device:TPU:1, one launch (start us, length us, event | category | flops | bytes accessed | tf_op | source)
XLA Modules:
  0.0 1907.4 jit_solution(8072526681034327603)
XLA Ops:
  6.5 41.8 %all_gather.6 = bf16[1,128,1024]{2,1,0:T(8,128)(2,1)} all-gather(bf16[1,8,1024]{2,1,0:T(8,128)(2,1)} %param.7), channel_id=1, replica_groups=mesh['src'=16,'tgt'=16] {'tgt'}, dimensions={1}, use_global_device_ids=true | all-gather | bytes 278528 | tf_op jit(solution)/shard_map/all_gather | solution.py:47
  49.1 42.1 %all-gather.2.cloned.1.call-done = bf16[16,128,1024]{2,1,0:T(8,128)(2,1)} async-done(((bf16[1,128,1024]{2,1,0:T(8,128)(2,1)}), bf16[16,128,1024]{2,1,0:T(8,128)(2,1)}) %all-gather.2.cloned.1.call-update) | async-done | bytes 4194320 | tf_op jit(solution)/shard_map/all_gather | solution.py:48
  91.2 3.4 fusion.309
  94.6 2.9 collective-permute-start
  97.5 1.9 collective-permute-start.1
  99.5 3.1 collective-permute-done.1
  102.6 4.5 collective-permute-start.2
  107.1 1.3 collective-permute-start.3
  108.9 4.5 collective-permute-done.3
  113.7 1786.3 %while.16 = (s32[]{:T(128)}, f32[2,2,16,128]{3,2,1,0:T(8,128)S(1)}, f32[8,81]{1,0:T(8,128)S(1)}, f32[8,81]{1,0:T(8,128)S(1)}, f32[6,6,18,130]{3,2,1,0:T(8,128)S(...) while((s32[]{:T(128)}, f32[2,2,16,128]{3,2,1,0:T(8,128)S(1)}, ...), condition=%wide.region_1.2_spmd.clone, body=%wide.region_0.1_spmd.clone.sunk | while | flops 13410323 | bytes 22420168 | solution.py:101
  117.9 53.1 %maximum_multiply_fusion.5 = f32[4,4,16,128]{3,2,1,0:T(8,128)S(1)} fusion(f32[6,6,18,130]{3,2,1,0:T(8,128)S(1)} %get-tuple-element.1378, f32[]{:T(128)} %bitcast.753, f32[]{:T(128)} %bitcast.754, f32[]{:T(128)} %bitcast.755, f32[]{:T(128)} %bitcast.756, f32[]{:T(128)} %bitcast.757, f32[]{:T(128)} %bitcast.758, f32[]{:T(128)} %bitcast.759, ...), kind=kLoop, calls=%fused_computation.145.clone.1 | loop fusion | flops 5373952 | bytes 10748296 | tf_op jit(solution)/shard_map/while/body/eval_jaxpr/mul | solution.py:89
  174.7 53.1 %maximum_multiply_fusion.4 = f32[4,4,16,128]{3,2,1,0:T(8,128)S(1)} fusion(f32[6,6,18,130]{3,2,1,0:T(8,128)S(1)} %get-tuple-element.1378, f32[4,4]{1,0:T(4,128)S(1)} %multiply_bitcast_fusion.2, f32[]{:T(128)} %bitcast.671, f32[]{:T(128)} %bitcast.672, f32[]{:T(128)} %bitcast.673, f32[]{:T(128)} %bitcast.674, f32[]{:T(128)} %bitcast.675, ...), kind=kLoop, calls=%fused_computation.146.clone.1 | loop fusion | flops 5373952 | bytes 10748296 | tf_op jit(solution)/shard_map/while/body/eval_jaxpr/mul | solution.py:85
  230.0 0.7 fusion.373
  231.5 0.7 fusion.376
  232.2 0.7 fusion.377
  233.0 0.7 fusion.378
  235.0 101.9 %fusion.380 = f32[2,2,16,128]{3,2,1,0:T(8,128)S(1)} fusion(f32[4,4,16,128]{3,2,1,0:T(8,128)S(1)} %maximum_multiply_fusion.4, f32[4,4,16,128]{3,2,1,0:T(8,128)S(1)} %maximum_multiply_fusion.5, f32[2,2,16,128]{3,2,1,0:T(8,128)S(1)} %get-tuple-element.1363, f32[]{:T(128)} %bitcast.834, f32[]{:T(128)} %bitcast.835, f32[]{:T(128)} %bitcast.836, ...), kind=kLoop, calls=%fused_computation.294.clone.1 | loop fusion | flops 2662400 | bytes 918153 | tf_op jit(solution)/shard_map/while/body/eval_jaxpr/add | solution.py:97
  341.2 53.1 %maximum_multiply_fusion.5 = f32[4,4,16,128]{3,2,1,0:T(8,128)S(1)} fusion(f32[6,6,18,130]{3,2,1,0:T(8,128)S(1)} %get-tuple-element.1378, f32[]{:T(128)} %bitcast.753, f32[]{:T(128)} %bitcast.754, f32[]{:T(128)} %bitcast.755, f32[]{:T(128)} %bitcast.756, f32[]{:T(128)} %bitcast.757, f32[]{:T(128)} %bitcast.758, f32[]{:T(128)} %bitcast.759, ...), kind=kLoop, calls=%fused_computation.145.clone.1 | loop fusion | flops 5373952 | bytes 10748296 | tf_op jit(solution)/shard_map/while/body/eval_jaxpr/mul | solution.py:89
  398.0 53.1 %maximum_multiply_fusion.4 = f32[4,4,16,128]{3,2,1,0:T(8,128)S(1)} fusion(f32[6,6,18,130]{3,2,1,0:T(8,128)S(1)} %get-tuple-element.1378, f32[4,4]{1,0:T(4,128)S(1)} %multiply_bitcast_fusion.2, f32[]{:T(128)} %bitcast.671, f32[]{:T(128)} %bitcast.672, f32[]{:T(128)} %bitcast.673, f32[]{:T(128)} %bitcast.674, f32[]{:T(128)} %bitcast.675, ...), kind=kLoop, calls=%fused_computation.146.clone.1 | loop fusion | flops 5373952 | bytes 10748296 | tf_op jit(solution)/shard_map/while/body/eval_jaxpr/mul | solution.py:85
  453.3 0.7 fusion.373
  454.8 0.7 fusion.376
  455.5 0.7 fusion.377
  456.2 0.7 fusion.378
  458.3 101.9 %fusion.380 = f32[2,2,16,128]{3,2,1,0:T(8,128)S(1)} fusion(f32[4,4,16,128]{3,2,1,0:T(8,128)S(1)} %maximum_multiply_fusion.4, f32[4,4,16,128]{3,2,1,0:T(8,128)S(1)} %maximum_multiply_fusion.5, f32[2,2,16,128]{3,2,1,0:T(8,128)S(1)} %get-tuple-element.1363, f32[]{:T(128)} %bitcast.834, f32[]{:T(128)} %bitcast.835, f32[]{:T(128)} %bitcast.836, ...), kind=kLoop, calls=%fused_computation.294.clone.1 | loop fusion | flops 2662400 | bytes 918153 | tf_op jit(solution)/shard_map/while/body/eval_jaxpr/add | solution.py:97
  564.5 53.1 %maximum_multiply_fusion.5 = f32[4,4,16,128]{3,2,1,0:T(8,128)S(1)} fusion(f32[6,6,18,130]{3,2,1,0:T(8,128)S(1)} %get-tuple-element.1378, f32[]{:T(128)} %bitcast.753, f32[]{:T(128)} %bitcast.754, f32[]{:T(128)} %bitcast.755, f32[]{:T(128)} %bitcast.756, f32[]{:T(128)} %bitcast.757, f32[]{:T(128)} %bitcast.758, f32[]{:T(128)} %bitcast.759, ...), kind=kLoop, calls=%fused_computation.145.clone.1 | loop fusion | flops 5373952 | bytes 10748296 | tf_op jit(solution)/shard_map/while/body/eval_jaxpr/mul | solution.py:89
  621.3 53.1 %maximum_multiply_fusion.4 = f32[4,4,16,128]{3,2,1,0:T(8,128)S(1)} fusion(f32[6,6,18,130]{3,2,1,0:T(8,128)S(1)} %get-tuple-element.1378, f32[4,4]{1,0:T(4,128)S(1)} %multiply_bitcast_fusion.2, f32[]{:T(128)} %bitcast.671, f32[]{:T(128)} %bitcast.672, f32[]{:T(128)} %bitcast.673, f32[]{:T(128)} %bitcast.674, f32[]{:T(128)} %bitcast.675, ...), kind=kLoop, calls=%fused_computation.146.clone.1 | loop fusion | flops 5373952 | bytes 10748296 | tf_op jit(solution)/shard_map/while/body/eval_jaxpr/mul | solution.py:85
  676.6 0.7 fusion.373
  678.0 0.7 fusion.376
  678.8 0.7 fusion.377
  679.5 0.7 fusion.378
  681.6 101.9 %fusion.380 = f32[2,2,16,128]{3,2,1,0:T(8,128)S(1)} fusion(f32[4,4,16,128]{3,2,1,0:T(8,128)S(1)} %maximum_multiply_fusion.4, f32[4,4,16,128]{3,2,1,0:T(8,128)S(1)} %maximum_multiply_fusion.5, f32[2,2,16,128]{3,2,1,0:T(8,128)S(1)} %get-tuple-element.1363, f32[]{:T(128)} %bitcast.834, f32[]{:T(128)} %bitcast.835, f32[]{:T(128)} %bitcast.836, ...), kind=kLoop, calls=%fused_computation.294.clone.1 | loop fusion | flops 2662400 | bytes 918153 | tf_op jit(solution)/shard_map/while/body/eval_jaxpr/add | solution.py:97
  787.8 53.1 %maximum_multiply_fusion.5 = f32[4,4,16,128]{3,2,1,0:T(8,128)S(1)} fusion(f32[6,6,18,130]{3,2,1,0:T(8,128)S(1)} %get-tuple-element.1378, f32[]{:T(128)} %bitcast.753, f32[]{:T(128)} %bitcast.754, f32[]{:T(128)} %bitcast.755, f32[]{:T(128)} %bitcast.756, f32[]{:T(128)} %bitcast.757, f32[]{:T(128)} %bitcast.758, f32[]{:T(128)} %bitcast.759, ...), kind=kLoop, calls=%fused_computation.145.clone.1 | loop fusion | flops 5373952 | bytes 10748296 | tf_op jit(solution)/shard_map/while/body/eval_jaxpr/mul | solution.py:89
  844.5 53.1 %maximum_multiply_fusion.4 = f32[4,4,16,128]{3,2,1,0:T(8,128)S(1)} fusion(f32[6,6,18,130]{3,2,1,0:T(8,128)S(1)} %get-tuple-element.1378, f32[4,4]{1,0:T(4,128)S(1)} %multiply_bitcast_fusion.2, f32[]{:T(128)} %bitcast.671, f32[]{:T(128)} %bitcast.672, f32[]{:T(128)} %bitcast.673, f32[]{:T(128)} %bitcast.674, f32[]{:T(128)} %bitcast.675, ...), kind=kLoop, calls=%fused_computation.146.clone.1 | loop fusion | flops 5373952 | bytes 10748296 | tf_op jit(solution)/shard_map/while/body/eval_jaxpr/mul | solution.py:85
  899.9 0.7 fusion.373
  901.3 0.7 fusion.376
  902.1 0.7 fusion.377
  902.8 0.7 fusion.378
  904.9 101.9 %fusion.380 = f32[2,2,16,128]{3,2,1,0:T(8,128)S(1)} fusion(f32[4,4,16,128]{3,2,1,0:T(8,128)S(1)} %maximum_multiply_fusion.4, f32[4,4,16,128]{3,2,1,0:T(8,128)S(1)} %maximum_multiply_fusion.5, f32[2,2,16,128]{3,2,1,0:T(8,128)S(1)} %get-tuple-element.1363, f32[]{:T(128)} %bitcast.834, f32[]{:T(128)} %bitcast.835, f32[]{:T(128)} %bitcast.836, ...), kind=kLoop, calls=%fused_computation.294.clone.1 | loop fusion | flops 2662400 | bytes 918153 | tf_op jit(solution)/shard_map/while/body/eval_jaxpr/add | solution.py:97
  1011.1 53.1 %maximum_multiply_fusion.5 = f32[4,4,16,128]{3,2,1,0:T(8,128)S(1)} fusion(f32[6,6,18,130]{3,2,1,0:T(8,128)S(1)} %get-tuple-element.1378, f32[]{:T(128)} %bitcast.753, f32[]{:T(128)} %bitcast.754, f32[]{:T(128)} %bitcast.755, f32[]{:T(128)} %bitcast.756, f32[]{:T(128)} %bitcast.757, f32[]{:T(128)} %bitcast.758, f32[]{:T(128)} %bitcast.759, ...), kind=kLoop, calls=%fused_computation.145.clone.1 | loop fusion | flops 5373952 | bytes 10748296 | tf_op jit(solution)/shard_map/while/body/eval_jaxpr/mul | solution.py:89
  1067.8 53.1 %maximum_multiply_fusion.4 = f32[4,4,16,128]{3,2,1,0:T(8,128)S(1)} fusion(f32[6,6,18,130]{3,2,1,0:T(8,128)S(1)} %get-tuple-element.1378, f32[4,4]{1,0:T(4,128)S(1)} %multiply_bitcast_fusion.2, f32[]{:T(128)} %bitcast.671, f32[]{:T(128)} %bitcast.672, f32[]{:T(128)} %bitcast.673, f32[]{:T(128)} %bitcast.674, f32[]{:T(128)} %bitcast.675, ...), kind=kLoop, calls=%fused_computation.146.clone.1 | loop fusion | flops 5373952 | bytes 10748296 | tf_op jit(solution)/shard_map/while/body/eval_jaxpr/mul | solution.py:85
  1123.2 0.7 fusion.373
  1124.6 0.7 fusion.376
  1125.4 0.7 fusion.377
  1126.1 0.7 fusion.378
  1128.2 101.9 %fusion.380 = f32[2,2,16,128]{3,2,1,0:T(8,128)S(1)} fusion(f32[4,4,16,128]{3,2,1,0:T(8,128)S(1)} %maximum_multiply_fusion.4, f32[4,4,16,128]{3,2,1,0:T(8,128)S(1)} %maximum_multiply_fusion.5, f32[2,2,16,128]{3,2,1,0:T(8,128)S(1)} %get-tuple-element.1363, f32[]{:T(128)} %bitcast.834, f32[]{:T(128)} %bitcast.835, f32[]{:T(128)} %bitcast.836, ...), kind=kLoop, calls=%fused_computation.294.clone.1 | loop fusion | flops 2662400 | bytes 918153 | tf_op jit(solution)/shard_map/while/body/eval_jaxpr/add | solution.py:97
  1234.4 53.1 %maximum_multiply_fusion.5 = f32[4,4,16,128]{3,2,1,0:T(8,128)S(1)} fusion(f32[6,6,18,130]{3,2,1,0:T(8,128)S(1)} %get-tuple-element.1378, f32[]{:T(128)} %bitcast.753, f32[]{:T(128)} %bitcast.754, f32[]{:T(128)} %bitcast.755, f32[]{:T(128)} %bitcast.756, f32[]{:T(128)} %bitcast.757, f32[]{:T(128)} %bitcast.758, f32[]{:T(128)} %bitcast.759, ...), kind=kLoop, calls=%fused_computation.145.clone.1 | loop fusion | flops 5373952 | bytes 10748296 | tf_op jit(solution)/shard_map/while/body/eval_jaxpr/mul | solution.py:89
  1291.1 53.1 %maximum_multiply_fusion.4 = f32[4,4,16,128]{3,2,1,0:T(8,128)S(1)} fusion(f32[6,6,18,130]{3,2,1,0:T(8,128)S(1)} %get-tuple-element.1378, f32[4,4]{1,0:T(4,128)S(1)} %multiply_bitcast_fusion.2, f32[]{:T(128)} %bitcast.671, f32[]{:T(128)} %bitcast.672, f32[]{:T(128)} %bitcast.673, f32[]{:T(128)} %bitcast.674, f32[]{:T(128)} %bitcast.675, ...), kind=kLoop, calls=%fused_computation.146.clone.1 | loop fusion | flops 5373952 | bytes 10748296 | tf_op jit(solution)/shard_map/while/body/eval_jaxpr/mul | solution.py:85
  1346.4 0.7 fusion.373
  1347.9 0.7 fusion.376
  1348.7 0.7 fusion.377
  1351.5 101.9 %fusion.380 = f32[2,2,16,128]{3,2,1,0:T(8,128)S(1)} fusion(f32[4,4,16,128]{3,2,1,0:T(8,128)S(1)} %maximum_multiply_fusion.4, f32[4,4,16,128]{3,2,1,0:T(8,128)S(1)} %maximum_multiply_fusion.5, f32[2,2,16,128]{3,2,1,0:T(8,128)S(1)} %get-tuple-element.1363, f32[]{:T(128)} %bitcast.834, f32[]{:T(128)} %bitcast.835, f32[]{:T(128)} %bitcast.836, ...), kind=kLoop, calls=%fused_computation.294.clone.1 | loop fusion | flops 2662400 | bytes 918153 | tf_op jit(solution)/shard_map/while/body/eval_jaxpr/add | solution.py:97
  1457.7 53.1 %maximum_multiply_fusion.5 = f32[4,4,16,128]{3,2,1,0:T(8,128)S(1)} fusion(f32[6,6,18,130]{3,2,1,0:T(8,128)S(1)} %get-tuple-element.1378, f32[]{:T(128)} %bitcast.753, f32[]{:T(128)} %bitcast.754, f32[]{:T(128)} %bitcast.755, f32[]{:T(128)} %bitcast.756, f32[]{:T(128)} %bitcast.757, f32[]{:T(128)} %bitcast.758, f32[]{:T(128)} %bitcast.759, ...), kind=kLoop, calls=%fused_computation.145.clone.1 | loop fusion | flops 5373952 | bytes 10748296 | tf_op jit(solution)/shard_map/while/body/eval_jaxpr/mul | solution.py:89
  1514.4 53.1 %maximum_multiply_fusion.4 = f32[4,4,16,128]{3,2,1,0:T(8,128)S(1)} fusion(f32[6,6,18,130]{3,2,1,0:T(8,128)S(1)} %get-tuple-element.1378, f32[4,4]{1,0:T(4,128)S(1)} %multiply_bitcast_fusion.2, f32[]{:T(128)} %bitcast.671, f32[]{:T(128)} %bitcast.672, f32[]{:T(128)} %bitcast.673, f32[]{:T(128)} %bitcast.674, f32[]{:T(128)} %bitcast.675, ...), kind=kLoop, calls=%fused_computation.146.clone.1 | loop fusion | flops 5373952 | bytes 10748296 | tf_op jit(solution)/shard_map/while/body/eval_jaxpr/mul | solution.py:85
  1569.7 0.7 fusion.373
  1571.2 0.7 fusion.376
  1571.9 0.7 fusion.377
  1572.7 0.7 fusion.378
  1574.8 101.9 %fusion.380 = f32[2,2,16,128]{3,2,1,0:T(8,128)S(1)} fusion(f32[4,4,16,128]{3,2,1,0:T(8,128)S(1)} %maximum_multiply_fusion.4, f32[4,4,16,128]{3,2,1,0:T(8,128)S(1)} %maximum_multiply_fusion.5, f32[2,2,16,128]{3,2,1,0:T(8,128)S(1)} %get-tuple-element.1363, f32[]{:T(128)} %bitcast.834, f32[]{:T(128)} %bitcast.835, f32[]{:T(128)} %bitcast.836, ...), kind=kLoop, calls=%fused_computation.294.clone.1 | loop fusion | flops 2662400 | bytes 918153 | tf_op jit(solution)/shard_map/while/body/eval_jaxpr/add | solution.py:97
  1681.0 53.1 %maximum_multiply_fusion.5 = f32[4,4,16,128]{3,2,1,0:T(8,128)S(1)} fusion(f32[6,6,18,130]{3,2,1,0:T(8,128)S(1)} %get-tuple-element.1378, f32[]{:T(128)} %bitcast.753, f32[]{:T(128)} %bitcast.754, f32[]{:T(128)} %bitcast.755, f32[]{:T(128)} %bitcast.756, f32[]{:T(128)} %bitcast.757, f32[]{:T(128)} %bitcast.758, f32[]{:T(128)} %bitcast.759, ...), kind=kLoop, calls=%fused_computation.145.clone.1 | loop fusion | flops 5373952 | bytes 10748296 | tf_op jit(solution)/shard_map/while/body/eval_jaxpr/mul | solution.py:89
  1737.7 53.1 %maximum_multiply_fusion.4 = f32[4,4,16,128]{3,2,1,0:T(8,128)S(1)} fusion(f32[6,6,18,130]{3,2,1,0:T(8,128)S(1)} %get-tuple-element.1378, f32[4,4]{1,0:T(4,128)S(1)} %multiply_bitcast_fusion.2, f32[]{:T(128)} %bitcast.671, f32[]{:T(128)} %bitcast.672, f32[]{:T(128)} %bitcast.673, f32[]{:T(128)} %bitcast.674, f32[]{:T(128)} %bitcast.675, ...), kind=kLoop, calls=%fused_computation.146.clone.1 | loop fusion | flops 5373952 | bytes 10748296 | tf_op jit(solution)/shard_map/while/body/eval_jaxpr/mul | solution.py:85
  1793.0 0.7 fusion.373
  1794.5 0.7 fusion.376
  1795.2 0.7 fusion.377
  1798.0 101.9 %fusion.380 = f32[2,2,16,128]{3,2,1,0:T(8,128)S(1)} fusion(f32[4,4,16,128]{3,2,1,0:T(8,128)S(1)} %maximum_multiply_fusion.4, f32[4,4,16,128]{3,2,1,0:T(8,128)S(1)} %maximum_multiply_fusion.5, f32[2,2,16,128]{3,2,1,0:T(8,128)S(1)} %get-tuple-element.1363, f32[]{:T(128)} %bitcast.834, f32[]{:T(128)} %bitcast.835, f32[]{:T(128)} %bitcast.836, ...), kind=kLoop, calls=%fused_computation.294.clone.1 | loop fusion | flops 2662400 | bytes 918153 | tf_op jit(solution)/shard_map/while/body/eval_jaxpr/add | solution.py:97
  (192 shorter events, 100.1 us)
Async XLA Ops:
  6.5 101.8 %copy-start.1 = (f32[8,81]{1,0:T(8,128)S(1)}, f32[8,81]{1,0:T(8,128)}, u32[]{:S(2)}) copy-start(f32[8,81]{1,0:T(8,128)} %param.11) | copy-start | bytes 7780
  6.5 102.1 %copy-start.2 = (f32[8,81]{1,0:T(8,128)S(1)}, f32[8,81]{1,0:T(8,128)}, u32[]{:S(2)}) copy-start(f32[8,81]{1,0:T(8,128)} %param.9) | copy-start | bytes 7780
  6.5 107.1 %copy-start.3 = (f32[8]{0:T(128)S(1)}, f32[8]{0:T(128)}, u32[]{:S(2)}) copy-start(f32[8]{0:T(128)} %param.10) | copy-start | bytes 100
  6.5 84.6 %all-gather.2.cloned.1.call-start = ((), (), s32[]{:S(2)}) async-start(), calls=%async_computation | async-start | bytes 4456448 | tf_op jit(solution)/shard_map/all_gather | solution.py:48
  94.6 4.9 collective-permute-start
  97.5 5.1 collective-permute-start.1
  102.6 6.3 collective-permute-start.2
  107.1 6.3 collective-permute-start.3
  1900.0 0.6 copy-start
Sparse Core Ops, SparseCore 0:
  48.5 42.6 all-gather.1
where the time goes:
time: 1930 us; the launch traced here: 1910 us
  other arithmetic  1670 us (87%)
  local copies, waits for them, and re-layouts  121 us (6%)
  waiting for transfers between devices  49.7 us (3%)
  blocking collectives  41.8 us (2%)
    add x8, other arithmetic, channel_step(): summed_total + filter_taps(jnp.pad(hidden_reflected, border_padding), ref...  815 us
    mul x16, other arithmetic, channel_step(): jax.nn.relu(filter_taps(field, conv_in[channel_slot], extended) + bias_in...  426 us
    mul x8, other arithmetic, channel_step(): jax.nn.relu(filter_taps(field, mirror_in[channel_slot], extended) + bias_...  425 us
    slice x160, local copies, waits for them, and re-layouts, filter_taps(): weight = weights[first * 27 + second * 9 + third * 3 + fourth]  115 us
    all_gather x1, waiting for transfers between devices, per_device(): piece = lax.all_gather(wide, 'src', axis=0, tiled=True)  42.1 us
    all_gather x1, blocking collectives, per_device(): wide = lax.all_gather(feature_a, 'tgt', axis=1, tiled=True)  41.8 us
  transfers between devices with their start and end apart: 5, of which 3 were waited for; matrix products, arithmetic and copies ran while one was open for 0% of the time, Pallas kernels for 0%

commit v1 on v0

v1 whole, which is shorter than its diff:
```python
import jax
import jax.numpy as jnp
import numpy as np
from jax import lax
from jax.experimental import pallas as pl
from jax.experimental.pallas import tpu as pltpu
from jax.sharding import PartitionSpec as P

SHIFTS = (-1, 0, 1)


def mirror_matrix():
    out = np.zeros((81, 81), np.float32)
    for p, q, r, s in np.ndindex(3, 3, 3, 3):
        out[27 * r + 9 * s + 3 * p + q, 27 * p + 9 * q + 3 * r + s] = 1
    return out


def spread_in():
    out = np.zeros((81, 2, 4, 256), np.float32)
    for k2, l, p, q, r, s in np.ndindex(2, 4, 3, 3, 3, 3):
        column = (s * 3 + r) * 24 + (l + q) // 2 * 8 + (k2 + p) * 2 + (l + q) % 2
        out[27 * p + 9 * q + 3 * r + s, k2, l, column] = 1
    return out.reshape(81, 2048)


def spread_out():
    out = np.zeros((81, 4, 4, 128), np.float32)
    for k2, l2, p, q, r, s in np.ndindex(2, 2, 3, 3, 3, 3):
        out[27 * p + 9 * q + 3 * r + s, k2 + p, l2 + q, (r * 3 + s) * 4 + k2 * 2 + l2] = 1
    return out.reshape(81, 2048)


def shifted(x, s):
    if s == 0:
        return x
    lane = lax.broadcasted_iota(jnp.int32, x.shape, 1)
    rolled = pltpu.roll(x, (-s) % 128, 1)
    return jnp.where(lane == (127 if s == 1 else 0), 0.0, rolled)


def weights_kernel(cin_ref, cout_ref, mirror_ref, sel1_ref, sel2_ref, w1_ref, w2_ref):
    def parts(x):
        high = x.astype(jnp.bfloat16)
        low = (x - high.astype(jnp.float32)).astype(jnp.bfloat16)
        rows = []
        for part in (high, low):
            rows.append(part.astype(jnp.float32))
            rows.append(jnp.dot(part, mirror_ref[...], preferred_element_type=jnp.float32))
        return jnp.concatenate(rows, axis=0).astype(jnp.bfloat16)

    t1 = jnp.dot(parts(cin_ref[...]), sel1_ref[...], preferred_element_type=jnp.float32)
    for hl in range(2):
        for kl in range(8):
            row = hl * 128 + kl * 16
            w1_ref[row : row + 16, :] = t1[
                hl * 16 : hl * 16 + 16, kl * 256 : kl * 256 + 256
            ].astype(jnp.bfloat16)
    t2 = jnp.dot(parts(cout_ref[...]), sel2_ref[...], preferred_element_type=jnp.float32)
    rows = []
    for hl in range(2):
        tall = jnp.concatenate(
            [t2[hl * 16 : hl * 16 + 16, kl * 128 : kl * 128 + 128] for kl in range(16)], axis=0
        )
        rows.append(tall.T[:40])
    w2_ref[...] = jnp.concatenate(rows, axis=0).astype(jnp.bfloat16)


def volume_kernel(b_ref, a_ref, o_ref, scr_ref):
    scores = lax.dot_general(
        b_ref[...], a_ref[...], (((1,), (1,)), ((), ())), preferred_element_type=jnp.float32
    ) * (1024 ** -0.5)
    zeros = jnp.zeros((12, 128), jnp.float32)
    scr_ref[0:12, :] = zeros
    scr_ref[204:216, :] = zeros
    for s in range(16):
        scr_ref[12 + 12 * s : 24 + 12 * s, :] = scores[16 * s : 16 * s + 12]
    for s in range(16):
        o_ref[s] = scr_ref[12 * s : 12 * s + 36, :].astype(jnp.bfloat16)


def consensus_kernel(r_ref, w1_ref, w2_ref, bias_ref, o_ref, rf_ref, xs_ref, ps_ref):
    zero_rows = jnp.zeros((24, 256), jnp.float32)
    for n in range(3):
        xs_ref[n, 0] = zero_rows
        xs_ref[n, 17] = zero_rows
    for i in range(16):
        rf_ref[i] = r_ref[i].astype(jnp.float32)
        for half in range(2):
            for ds in range(3):
                rows = rf_ref[i, pl.ds(ds * 12 + half * 4, 8), :]
                for n, s in enumerate(SHIFTS):
                    xs_ref[n, i + 1, ds * 8 : ds * 8 + 8, half * 128 : half * 128 + 128] = shifted(
                        rows, s
                    )
    ps_ref[0:40, :] = jnp.zeros((40, 128), jnp.float32)
    ps_ref[680:720, :] = jnp.zeros((40, 128), jnp.float32)
    pad = jnp.zeros((40, 256), jnp.float32)
    for i in range(0, 16, 2):
        highs, lows = [], []
        for d in range(2):
            rhs = jnp.concatenate(
                [xs_ref[n, i + d + r] for n in range(3) for r in range(3)] + [pad], axis=0
            ).astype(jnp.bfloat16)
            acc = jnp.dot(w1_ref[...], rhs, preferred_element_type=jnp.float32)
            acc = acc[:128] + acc[128:]
            hidden = jnp.concatenate([acc[:, :128], acc[:, 128:]], axis=0)
            hidden = jnp.maximum(hidden + bias_ref[...], 0.0)
            high = hidden.astype(jnp.bfloat16)
            highs.append(high)
            lows.append((hidden - high.astype(jnp.float32)).astype(jnp.bfloat16))
        both = jnp.dot(
            w2_ref[...], jnp.concatenate(highs, axis=1), preferred_element_type=jnp.float32
        )
        more = jnp.dot(
            w2_ref[0:40, :], jnp.concatenate(lows, axis=1), preferred_element_type=jnp.float32
        )
        total = both[:40] + both[40:] + more
        ps_ref[40 * (i + 1) : 40 * (i + 2), :] = total[:, :128]
        ps_ref[40 * (i + 2) : 40 * (i + 3), :] = total[:, 128:]
    for kl in range(4):
        out = None
        for n, s in enumerate(SHIFTS):
            part = None
            for r in range(3):
                rows = ps_ref[pl.ds(40 * r + (r * 3 + n) * 4 + kl, 16, stride=40), :]
                part = rows if part is None else part + rows
            part = shifted(part, s)
            out = part if out is None else out + part
        o_ref[kl * 16 : kl * 16 + 16, :] = out


VMEM = pl.BlockSpec(memory_space=pltpu.VMEM)


def call(kernel, outs, scratch, flops, *args):
    return pl.pallas_call(
        kernel,
        out_shape=outs,
        in_specs=[VMEM] * len(args),
        out_specs=jax.tree.map(lambda _: VMEM, outs),
        scratch_shapes=scratch,
        compiler_params=pltpu.CompilerParams(vmem_limit_bytes=16 << 20),
        cost_estimate=pl.CostEstimate(flops=flops, bytes_accessed=1 << 20, transcendentals=0),
    )(*args)


def per_device(feature_a, feature_b, conv_in, bias_in, conv_out):
    count = lax.axis_size("tgt")
    up = [(i, i + 1) for i in range(count - 1)]
    down = [(i + 1, i) for i in range(count - 1)]
    low = lax.ppermute(feature_b, "tgt", up)
    high = lax.ppermute(feature_b, "tgt", down)
    wide = lax.all_to_all(
        jnp.broadcast_to(feature_a, (16, 8, 1024)), "tgt", 0, 0, tiled=True
    ).reshape(128, 1024)
    tall = jnp.concatenate([low, feature_b, high, jnp.zeros_like(feature_b)], axis=0)
    tall = lax.all_to_all(
        jnp.broadcast_to(tall.reshape(1, 16, 1024), (16, 16, 1024)), "src", 0, 0, tiled=True
    ).reshape(256, 1024)
    w1, w2 = call(
        weights_kernel,
        (
            jax.ShapeDtypeStruct((256, 256), jnp.bfloat16),
            jax.ShapeDtypeStruct((80, 256), jnp.bfloat16),
        ),
        [],
        1 << 24,
        conv_in,
        conv_out,
        jnp.asarray(mirror_matrix(), jnp.bfloat16),
        jnp.asarray(spread_in(), jnp.bfloat16),
        jnp.asarray(spread_out(), jnp.bfloat16),
    )
    row = lax.axis_index("tgt") * 2 - 1 + jnp.arange(4)
    column = lax.axis_index("src") * 2 - 1 + jnp.arange(4)
    inside = ((row >= 0) & (row < 32))[:, None] & ((column >= 0) & (column < 32))[None, :]
    bias = jnp.where(
        inside[:, :, None, None, None], bias_in[None, None, None, :, None], -1e30
    )
    bias = jnp.broadcast_to(bias, (4, 4, 2, 8, 128)).reshape(256, 128)
    pieces = call(
        volume_kernel,
        jax.ShapeDtypeStruct((16, 36, 128), jnp.bfloat16),
        [pltpu.VMEM((216, 128), jnp.float32)],
        1 << 26,
        tall,
        wide,
    )
    pieces = lax.all_to_all(pieces, "src", 0, 0, tiled=True)
    out = call(
        consensus_kernel,
        jax.ShapeDtypeStruct((64, 128), jnp.float32),
        [
            pltpu.VMEM((16, 36, 128), jnp.float32),
            pltpu.VMEM((3, 18, 24, 256), jnp.float32),
            pltpu.VMEM((720, 128), jnp.float32),
        ],
        1 << 28,
        pieces,
        w1,
        w2,
        bias,
    )
    return out.reshape(2, 2, 16, 128)


def solution(mesh):
    in_specs = (P("src", "tgt", None), P("tgt", "src", None), P(), P(), P())
    out_specs = P("tgt", "src", None, None)
    return jax.shard_map(
        per_device, mesh=mesh, in_specs=in_specs, out_specs=out_specs, check_vma=False
    )
```

time: 1930 us -> 58.5 us (0.03); the launches traced: 1910 us -> 58 us
  other arithmetic: 1670 us -> 0.25 us
  local copies, waits for them, and re-layouts: 121 us -> 3.16 us
  blocking collectives: 41.8 us -> 0 us
  waiting for transfers between devices: 49.7 us -> 19.5 us
  starting transfers between devices: 10.6 us -> 30.3 us
    mul x24 -> x0, other arithmetic: 851 us -> none  [the longest x16 426 us: channel_step(): jax.nn.relu(filter_taps(field, conv_in[channel_slot], extended) + bias_in...]
    add x8 -> x0, other arithmetic: 815 us -> none  [channel_step(): summed_total + filter_taps(jnp.pad(hidden_reflected, border_padding), ref...]
    slice x160 -> x0, local copies, waits for them, and re-layouts: 115 us -> none  [filter_taps(): weight = weights[first * 27 + second * 9 + third * 3 + fourth]]
    all_gather x1 -> x0, waiting for transfers between devices: 42.1 us -> none  [per_device(): piece = lax.all_gather(wide, 'src', axis=0, tiled=True)]
    all_gather x1 -> x0, blocking collectives: 41.8 us -> none  [per_device(): wide = lax.all_gather(feature_a, 'tgt', axis=1, tiled=True)]
    all_to_all x0 -> x3, starting transfers between devices: none -> 23.5 us  [the longest x1 11.9 us: per_device(): lax.all_to_all(jnp.broadcast_to(feature_a, (16, 8, 1024)), 'tgt', 0, 0, t...]
  transfers between devices with their start and end apart: 5 -> 5, of which waited for: 3 -> 4; matrix products, arithmetic and copies ran while one was open for 0% -> 1% of each run, Pallas kernels for 0% -> 1%
where the time goes in v1:
time: 58.5 us; the launch traced here: 58 us
  starting transfers between devices  30.3 us (52%)
  waiting for transfers between devices  19.5 us (33%)
  Pallas kernels  4.59 us (8%)
  local copies, waits for them, and re-layouts  3.16 us (5%)
    all_to_all x1, starting transfers between devices, per_device(): lax.all_to_all(jnp.broadcast_to(feature_a, (16, 8, 1024)), 'tgt', 0, 0, t...  11.9 us
    all_to_all x1, waiting for transfers between devices, per_device(): lax.all_to_all(jnp.broadcast_to(tall.reshape(1, 16, 1024), (16, 16, 1024)...  9.41 us
    all_to_all x1, starting transfers between devices, per_device(): lax.all_to_all(jnp.broadcast_to(tall.reshape(1, 16, 1024), (16, 16, 1024)...  6.79 us
    ppermute x1, starting transfers between devices, per_device(): low = lax.ppermute(feature_b, 'tgt', up)  5.49 us
    all_to_all x1, waiting for transfers between devices, per_device(): pieces = lax.all_to_all(pieces, 'src', 0, 0, tiled=True)  5.06 us
    all_to_all x1, starting transfers between devices, per_device(): pieces = lax.all_to_all(pieces, 'src', 0, 0, tiled=True)  4.87 us
    pallas_call x3, Pallas kernels, call(): pl.pallas_call(kernel, out_shape=outs, in_specs=[VMEM] * len(args), out_s...  4.59 us
    all_to_all x1, waiting for transfers between devices, per_device(): lax.all_to_all(jnp.broadcast_to(feature_a, (16, 8, 1024)), 'tgt', 0, 0, t...  4.37 us
  transfers between devices with their start and end apart: 5, of which 4 were waited for; matrix products, arithmetic and copies ran while one was open for 1% of the time, Pallas kernels for 1%

profile of v1, /device:TPU:1, one launch (start us, length us, event | category | flops | bytes accessed | tf_op | source)
XLA Modules:
  0.0 58.0 jit_solution(14708153244298936889)
XLA Ops:
  0.0 1.4 %broadcast_in_dim.54 = bf16[16,8,1024]{2,1,0:T(8,128)(2,1)} broadcast(bf16[8,1024]{1,0:T(8,128)(2,1)} %bitcast.6), dimensions={1,2} | broadcast | bytes 278528 | tf_op jit(solution)/shard_map/broadcast_in_dim | solution.py:155
  1.4 0.0 copy-start.5
  1.4 11.9 %all-to-all-start.1 = ((bf16[16,8,1024]{2,1,0:T(8,128)(2,1)}), bf16[16,8,1024]{2,1,0:T(8,128)(2,1)S(1)}, u32[]{:S(2)}, u32[]{:S(2)}) async-start(bf16[16,8,1024]{2,1,0:T(8,128)(2,1)} %broadcast_in_dim.54), calls=%async_computation.1 | async-start | bytes 524288 | tf_op jit(solution)/shard_map/all_to_all | solution.py:154
  13.3 0.0 copy-done.5
  13.3 1.3 %collective-permute-start.1 = (bf16[2,2,1024]{2,1,0:T(2,128)(2,1)S(1)}, bf16[2,2,1024]{2,1,0:T(2,128)(2,1)S(1)}, u32[]{:S(2)}, u32[]{:S(2)}) collective-permute-start(bf16[2,2,1024]{2,1,0:T(2,128)(2,1)S(1)} %copy-done.5), channel_id=1, source_target_pairs={{1,0},{2,1},{3,2},{4,3},{5,4},{6,5},{7,6},{8,7},{9,8},{10,9},{11,1... | collective-permute-start | bytes 24584 | tf_op jit(solution)/shard_map/ppermute | solution.py:153
  14.6 5.5 %collective-permute-start = (bf16[2,2,1024]{2,1,0:T(2,128)(2,1)S(1)}, bf16[2,2,1024]{2,1,0:T(2,128)(2,1)S(1)}, u32[]{:S(2)}, u32[]{:S(2)}) collective-permute-start(bf16[2,2,1024]{2,1,0:T(2,128)(2,1)S(1)} %copy-done.5), channel_id=1, source_target_pairs={{0,1},{1,2},{2,3},{3,4},{4,5},{5,6},{6,7},{7,8},{8,9},{9,10},{10,1... | collective-permute-start | bytes 24584 | tf_op jit(solution)/shard_map/ppermute | solution.py:152
  20.1 0.1 pad.3.clone
  20.2 0.0 collective-permute-done.1
  20.2 0.7 %collective-permute-done = bf16[2,2,1024]{2,1,0:T(2,128)(2,1)S(1)} collective-permute-done((bf16[2,2,1024]{2,1,0:T(2,128)(2,1)S(1)}, bf16[2,2,1024]{2,1,0:T(2,128)(2,1)S(1)}, u32[]{:S(2)}, u32[]{:S(2)}) %collective-permute-start) | collective-permute-done | bytes 8224 | tf_op jit(solution)/shard_map/ppermute | solution.py:152
  20.9 0.1 maximum_maximum_fusion
  21.0 4.4 %all-to-all-done.1 = bf16[16,8,1024]{2,1,0:T(8,128)(2,1)S(1)} async-done(((bf16[16,8,1024]{2,1,0:T(8,128)(2,1)}), bf16[16,8,1024]{2,1,0:T(8,128)(2,1)S(1)}, u32[]{:S(2)}, u32[]{:S(2)}) %all-to-all-start.1) | async-done | bytes 262176 | tf_op jit(solution)/shard_map/all_to_all | solution.py:154
  25.4 0.9 %broadcast_in_dim.52 = bf16[16,16,1024]{2,1,0:T(8,128)(2,1)} broadcast(bf16[16,1024]{1,0:T(8,128)(2,1)S(1)} %broadcast_in_dim.51), dimensions={1,2} | broadcast | bytes 557056 | tf_op jit(solution)/shard_map/broadcast_in_dim | solution.py:159
  26.2 6.8 %all-to-all-start = ((bf16[16,16,1024]{2,1,0:T(8,128)(2,1)}), bf16[16,16,1024]{2,1,0:T(8,128)(2,1)S(1)}, u32[]{:S(2)}, u32[]{:S(2)}) async-start(bf16[16,16,1024]{2,1,0:T(8,128)(2,1)} %broadcast_in_dim.52), calls=%async_computation | async-start | bytes 1048576 | tf_op jit(solution)/shard_map/all_to_all | solution.py:158
  33.0 0.1 broadcast_and_fusion
  33.1 9.4 %all-to-all-done = bf16[16,16,1024]{2,1,0:T(8,128)(2,1)S(1)} async-done(((bf16[16,16,1024]{2,1,0:T(8,128)(2,1)}), bf16[16,16,1024]{2,1,0:T(8,128)(2,1)S(1)}, u32[]{:S(2)}, u32[]{:S(2)}) %all-to-all-start) | async-done | bytes 524320 | tf_op jit(solution)/shard_map/all_to_all | solution.py:158
  42.5 0.0 copy-start.6
  42.5 0.0 copy-start.1
  42.5 0.0 copy-start.2
  42.5 1.0 %shard_map.82 = bf16[16,36,128]{2,1,0:T(8,128)(2,1)} custom-call(bf16[256,1024]{1,0:T(8,128)(2,1)S(1)} %bitcast.4, bf16[128,1024]{1,0:T(8,128)(2,1)S(1)} %bitcast.5), custom_call_target="tpu_custom_call" | custom-call | flops 67108864 | bytes 1048576 | tf_op jit(solution)/shard_map/pallas_call | solution.py:137
  43.5 0.0 copy-start
  43.5 4.9 %all-to-all-start.2 = ((bf16[16,36,128]{2,1,0:T(8,128)(2,1)}), bf16[16,36,128]{2,1,0:T(8,128)(2,1)S(1)}, u32[]{:S(2)}, u32[]{:S(2)}) async-start(bf16[16,36,128]{2,1,0:T(8,128)(2,1)} %shard_map.82), calls=%async_computation.2 | async-start | bytes 327680 | tf_op jit(solution)/shard_map/all_to_all | solution.py:190
  48.4 0.0 copy-done.6
  48.4 0.1 broadcast_select_fusion
  48.5 0.0 copy-start.3
  48.5 0.0 copy-start.4
  48.5 0.1 broadcast_in_dim.59
  48.6 0.0 copy-done.1
  48.6 0.0 copy-done.2
  48.6 0.0 copy-done
  48.7 0.5 copy-done.3
  49.2 0.0 copy-done.4
  49.2 0.5 shard_map.83
  49.8 5.1 %all-to-all-done.2.r_ref = bf16[16,36,128]{2,1,0:T(8,128)(2,1)S(1)} async-done(((bf16[16,36,128]{2,1,0:T(8,128)(2,1)}), bf16[16,36,128]{2,1,0:T(8,128)(2,1)S(1)}, u32[]{:S(2)}, u32[]{:S(2)}) %all-to-all-start.2) | async-done | bytes 147488 | tf_op jit(solution)/shard_map/all_to_all | solution.py:190
  54.8 0.1 broadcast_in_dim.60.bias_ref
  54.9 3.0 %shard_map.84 = f32[64,128]{1,0:T(8,128)} custom-call(bf16[16,36,128]{2,1,0:T(8,128)(2,1)S(1)} %all-to-all-done.2.r_ref, bf16[256,256]{1,0:T(8,128)(2,1)S(1)} %get-tuple-element.7.w1_ref, bf16[80,256]{1,0:T(8,128)(2,1)S(1)} %get-tuple-element.8.w2_ref, f32[256,128]{1,0:T(8,128)S(1)} %broadcast_in_dim.60.bias_ref), custom_call_target="tpu_custom_call" | custom-call | flops 268435456 | bytes 1048576 | tf_op jit(solution)/shard_map/pallas_call | solution.py:137
  (4 shorter events, 0.0 us)
Async XLA Ops:
  1.4 11.9 %copy-start.5 = (bf16[2,2,1024]{2,1,0:T(2,128)(2,1)S(1)}, bf16[2,2,1024]{2,1,0:T(2,128)(2,1)}, u32[]{:S(2)}) copy-start(bf16[2,2,1024]{2,1,0:T(2,128)(2,1)} %param.9) | copy-start | bytes 24580
  1.4 24.0 %all-to-all-start.1 = ((bf16[16,8,1024]{2,1,0:T(8,128)(2,1)}), bf16[16,8,1024]{2,1,0:T(8,128)(2,1)S(1)}, u32[]{:S(2)}, u32[]{:S(2)}) async-start(bf16[16,8,1024]{2,1,0:T(8,128)(2,1)} %broadcast_in_dim.54), calls=%async_computation.1 | async-start | bytes 524288 | tf_op jit(solution)/shard_map/all_to_all | solution.py:154
  13.3 6.9 %collective-permute-start.1 = (bf16[2,2,1024]{2,1,0:T(2,128)(2,1)S(1)}, bf16[2,2,1024]{2,1,0:T(2,128)(2,1)S(1)}, u32[]{:S(2)}, u32[]{:S(2)}) collective-permute-start(bf16[2,2,1024]{2,1,0:T(2,128)(2,1)S(1)} %copy-done.5), channel_id=1, source_target_pairs={{1,0},{2,1},{3,2},{4,3},{5,4},{6,5},{7,6},{8,7},{9,8},{10,9},{11,1... | collective-permute-start | bytes 24584 | tf_op jit(solution)/shard_map/ppermute | solution.py:153
  14.6 6.3 %collective-permute-start = (bf16[2,2,1024]{2,1,0:T(2,128)(2,1)S(1)}, bf16[2,2,1024]{2,1,0:T(2,128)(2,1)S(1)}, u32[]{:S(2)}, u32[]{:S(2)}) collective-permute-start(bf16[2,2,1024]{2,1,0:T(2,128)(2,1)S(1)} %copy-done.5), channel_id=1, source_target_pairs={{0,1},{1,2},{2,3},{3,4},{4,5},{5,6},{6,7},{7,8},{8,9},{9,10},{10,1... | collective-permute-start | bytes 24584 | tf_op jit(solution)/shard_map/ppermute | solution.py:152
  26.2 16.3 %all-to-all-start = ((bf16[16,16,1024]{2,1,0:T(8,128)(2,1)}), bf16[16,16,1024]{2,1,0:T(8,128)(2,1)S(1)}, u32[]{:S(2)}, u32[]{:S(2)}) async-start(bf16[16,16,1024]{2,1,0:T(8,128)(2,1)} %broadcast_in_dim.52), calls=%async_computation | async-start | bytes 1048576 | tf_op jit(solution)/shard_map/all_to_all | solution.py:158
  42.5 5.9 %copy-start.6 = (f32[8]{0:T(128)S(1)}, f32[8]{0:T(128)}, u32[]{:S(2)}) copy-start(f32[8]{0:T(128)} %param.11) | copy-start | bytes 100
  42.5 6.1 %copy-start.1 = (bf16[81,2048]{1,0:T(8,128)(2,1)S(1)}, bf16[81,2048]{1,0:T(8,128)(2,1)}, u32[]{:S(2)}) copy-start(bf16[81,2048]{1,0:T(8,128)(2,1)} %constant.29.clone.sel2_ref) | copy-start | bytes 995332
  42.5 6.1 %copy-start.2 = (bf16[81,81]{1,0:T(8,128)(2,1)S(1)}, bf16[81,81]{1,0:T(8,128)(2,1)}, u32[]{:S(2)}) copy-start(bf16[81,81]{1,0:T(8,128)(2,1)} %constant.27.clone.mirror_ref) | copy-start | bytes 39370
  43.5 5.1 %copy-start = (bf16[81,2048]{1,0:T(8,128)(2,1)S(1)}, bf16[81,2048]{1,0:T(8,128)(2,1)}, u32[]{:S(2)}) copy-start(bf16[81,2048]{1,0:T(8,128)(2,1)} %constant.28.clone.sel1_ref) | copy-start | bytes 995332
  43.5 11.3 %all-to-all-start.2 = ((bf16[16,36,128]{2,1,0:T(8,128)(2,1)}), bf16[16,36,128]{2,1,0:T(8,128)(2,1)S(1)}, u32[]{:S(2)}, u32[]{:S(2)}) async-start(bf16[16,36,128]{2,1,0:T(8,128)(2,1)} %shard_map.82), calls=%async_computation.2 | async-start | bytes 327680 | tf_op jit(solution)/shard_map/all_to_all | solution.py:190
  48.5 0.7 %copy-start.3 = (f32[8,81]{1,0:T(8,128)S(1)}, f32[8,81]{1,0:T(8,128)}, u32[]{:S(2)}) copy-start(f32[8,81]{1,0:T(8,128)} %cin_ref.1) | copy-start | bytes 7780
  48.5 0.7 %copy-start.4 = (f32[8,81]{1,0:T(8,128)S(1)}, f32[8,81]{1,0:T(8,128)}, u32[]{:S(2)}) copy-start(f32[8,81]{1,0:T(8,128)} %cout_ref.1) | copy-start | bytes 7780

commit v2 on v1

--- a/solution.py
+++ b/solution.py
@@ -19,7 +19,8 @@
 def spread_in():
     out = np.zeros((81, 2, 4, 256), np.float32)
     for k2, l, p, q, r, s in np.ndindex(2, 4, 3, 3, 3, 3):
-        column = (s * 3 + r) * 24 + (l + q) // 2 * 8 + (k2 + p) * 2 + (l + q) % 2
+        k, c = k2 + p, l + q
+        column = (s * 3 + r) * 24 + k // 2 * 12 + c // 2 * 4 + k % 2 * 2 + c % 2
         out[27 * p + 9 * q + 3 * r + s, k2, l, column] = 1
     return out.reshape(81, 2048)
 
@@ -66,17 +67,20 @@
     w2_ref[...] = jnp.concatenate(rows, axis=0).astype(jnp.bfloat16)
 
 
-def volume_kernel(b_ref, a_ref, o_ref, scr_ref):
+def volume_kernel(low_ref, own_ref, high_ref, a_ref, o_ref, scr_ref, tmp_ref):
+    tall = jnp.concatenate([low_ref[...], own_ref[...], high_ref[...]], axis=0)
     scores = lax.dot_general(
-        b_ref[...], a_ref[...], (((1,), (1,)), ((), ())), preferred_element_type=jnp.float32
+        tall, a_ref[...], (((1,), (1,)), ((), ())), preferred_element_type=jnp.float32
     ) * (1024 ** -0.5)
-    zeros = jnp.zeros((12, 128), jnp.float32)
-    scr_ref[0:12, :] = zeros
-    scr_ref[204:216, :] = zeros
+    zeros = jnp.zeros((8, 128), jnp.float32)
+    for n in range(3):
+        scr_ref[n, 0:8, :] = zeros
+        scr_ref[n, 8:72, :] = scores[64 * n : 64 * n + 64]
+        scr_ref[n, 72:80, :] = zeros
     for s in range(16):
-        scr_ref[12 + 12 * s : 24 + 12 * s, :] = scores[16 * s : 16 * s + 12]
-    for s in range(16):
-        o_ref[s] = scr_ref[12 * s : 12 * s + 36, :].astype(jnp.bfloat16)
+        for n in range(3):
+            tmp_ref[s, 12 * n : 12 * n + 12, :] = scr_ref[n, 4 + 4 * s : 16 + 4 * s, :]
+        o_ref[s] = tmp_ref[s, 0:36, :].astype(jnp.bfloat16)
 
 
 def consensus_kernel(r_ref, w1_ref, w2_ref, bias_ref, o_ref, rf_ref, xs_ref, ps_ref):
@@ -87,12 +91,10 @@
     for i in range(16):
         rf_ref[i] = r_ref[i].astype(jnp.float32)
         for half in range(2):
-            for ds in range(3):
-                rows = rf_ref[i, pl.ds(ds * 12 + half * 4, 8), :]
+            for d in range(0, 24, 8):
+                rows = rf_ref[i, pl.ds(half * 12 + d, 8), :]
                 for n, s in enumerate(SHIFTS):
-                    xs_ref[n, i + 1, ds * 8 : ds * 8 + 8, half * 128 : half * 128 + 128] = shifted(
-                        rows, s
-                    )
+                    xs_ref[n, i + 1, d : d + 8, half * 128 : half * 128 + 128] = shifted(rows, s)
     ps_ref[0:40, :] = jnp.zeros((40, 128), jnp.float32)
     ps_ref[680:720, :] = jnp.zeros((40, 128), jnp.float32)
     pad = jnp.zeros((40, 256), jnp.float32)
@@ -146,18 +148,21 @@
 
 
 def per_device(feature_a, feature_b, conv_in, bias_in, conv_out):
-    count = lax.axis_size("tgt")
-    up = [(i, i + 1) for i in range(count - 1)]
-    down = [(i + 1, i) for i in range(count - 1)]
-    low = lax.ppermute(feature_b, "tgt", up)
-    high = lax.ppermute(feature_b, "tgt", down)
+    b = lax.all_to_all(
+        jnp.broadcast_to(feature_b.reshape(1, 4, 1024), (16, 4, 1024)), "src", 0, 0, tiled=True
+    ).reshape(64, 1024)
+    other = lax.ppermute(feature_a, "yh", [(0, 1), (1, 0)])
+    first = lax.axis_index("yh") == 0
+    wide = jnp.concatenate(
+        [jnp.where(first, feature_a, other), jnp.where(first, other, feature_a)], axis=1
+    )
     wide = lax.all_to_all(
-        jnp.broadcast_to(feature_a, (16, 8, 1024)), "tgt", 0, 0, tiled=True
+        jnp.broadcast_to(wide, (8, 16, 1024)), "z", 0, 0, tiled=True
     ).reshape(128, 1024)
-    tall = jnp.concatenate([low, feature_b, high, jnp.zeros_like(feature_b)], axis=0)
-    tall = lax.all_to_all(
-        jnp.broadcast_to(tall.reshape(1, 16, 1024), (16, 16, 1024)), "src", 0, 0, tiled=True
-    ).reshape(256, 1024)
+    up = [(i, i + 1) for i in range(15)]
+    down = [(i + 1, i) for i in range(15)]
+    low = lax.ppermute(b, ("z", "yh"), up)
+    high = lax.ppermute(b, ("z", "yh"), down)
     w1, w2 = call(
         weights_kernel,
         (
@@ -172,7 +177,7 @@
         jnp.asarray(spread_in(), jnp.bfloat16),
         jnp.asarray(spread_out(), jnp.bfloat16),
     )
-    row = lax.axis_index("tgt") * 2 - 1 + jnp.arange(4)
+    row = lax.axis_index(("z", "yh")) * 2 - 1 + jnp.arange(4)
     column = lax.axis_index("src") * 2 - 1 + jnp.arange(4)
     inside = ((row >= 0) & (row < 32))[:, None] & ((column >= 0) & (column < 32))[None, :]
     bias = jnp.where(
@@ -182,9 +187,11 @@
     pieces = call(
         volume_kernel,
         jax.ShapeDtypeStruct((16, 36, 128), jnp.bfloat16),
-        [pltpu.VMEM((216, 128), jnp.float32)],
+        [pltpu.VMEM((3, 80, 128), jnp.float32), pltpu.VMEM((16, 40, 128), jnp.float32)],
         1 << 26,
-        tall,
+        low,
+        b,
+        high,
         wide,
     )
     pieces = lax.all_to_all(pieces, "src", 0, 0, tiled=True)
@@ -206,8 +213,10 @@
 
 
 def solution(mesh):
-    in_specs = (P("src", "tgt", None), P("tgt", "src", None), P(), P(), P())
-    out_specs = P("tgt", "src", None, None)
+    mesh = jax.sharding.Mesh(mesh.devices.reshape(16, 8, 2), ("src", "z", "yh"))
+    tgt = ("z", "yh")
+    in_specs = (P("src", tgt, None), P(tgt, "src", None), P(), P(), P())
+    out_specs = P(tgt, "src", None, None)
     return jax.shard_map(
         per_device, mesh=mesh, in_specs=in_specs, out_specs=out_specs, check_vma=False
     )

time: 58.5 us -> 54.2 us (0.926)
  the two profiles are of different devices: /device:TPU:1 before, /device:TPU:113 now
where the time goes in v2:
time: 54.2 us; the launch traced here: 53.7 us
  starting transfers between devices  27.5 us (51%)
  waiting for transfers between devices  18.4 us (34%)
  Pallas kernels  4.55 us (8%)
  local copies, waits for them, and re-layouts  2.96 us (5%)
    all_to_all x1, starting transfers between devices, per_device(): lax.all_to_all(jnp.broadcast_to(wide, (8, 16, 1024)), 'z', 0, 0, tiled=True)  7.1 us
    all_to_all x1, starting transfers between devices, per_device(): lax.all_to_all(jnp.broadcast_to(feature_b.reshape(1, 4, 1024), (16, 4, 10...  7.02 us
    ppermute x1, waiting for transfers between devices, per_device(): high = lax.ppermute(b, ('z', 'yh'), down)  6.86 us
    all_to_all x1, waiting for transfers between devices, per_device(): lax.all_to_all(jnp.broadcast_to(feature_b.reshape(1, 4, 1024), (16, 4, 10...  6.01 us
    all_to_all x1, starting transfers between devices, per_device(): pieces = lax.all_to_all(pieces, 'src', 0, 0, tiled=True)  5.95 us
    ppermute x1, starting transfers between devices, per_device(): low = lax.ppermute(b, ('z', 'yh'), up)  5.43 us
    all_to_all x1, waiting for transfers between devices, per_device(): pieces = lax.all_to_all(pieces, 'src', 0, 0, tiled=True)  5.06 us
    pallas_call x3, Pallas kernels, call(): pl.pallas_call(kernel, out_shape=outs, in_specs=[VMEM] * len(args), out_s...  4.55 us
  transfers between devices with their start and end apart: 6, of which 4 were waited for; matrix products, arithmetic and copies ran while one was open for 3% of the time, Pallas kernels for 1%

profile of v2, /device:TPU:113, one launch (start us, length us, event | category | flops | bytes accessed | tf_op | source)
XLA Modules:
  0.0 53.7 jit_solution(8325373139281838113)
XLA Ops:
  0.0 0.1 collective-permute-start.2
  0.1 0.7 %broadcast_in_dim.47 = bf16[4,1024]{1,0:T(4,128)(2,1)S(1)} reshape(bf16[2,2,1024]{2,1,0:T(2,128)(2,1)} %param.9) | data formatting | bytes 16384 | tf_op jit(solution)/shard_map/broadcast_in_dim | solution.py:152
  0.8 0.7 %broadcast_in_dim.48 = bf16[16,4,1024]{2,1,0:T(4,128)(2,1)} broadcast(bf16[4,1024]{1,0:T(4,128)(2,1)S(1)} %broadcast_in_dim.47), dimensions={1,2} | broadcast | bytes 139264 | tf_op jit(solution)/shard_map/broadcast_in_dim | solution.py:152
  1.5 0.0 copy-start.5
  1.5 7.0 %all-to-all-start = ((bf16[16,4,1024]{2,1,0:T(4,128)(2,1)}), bf16[16,4,1024]{2,1,0:T(4,128)(2,1)S(1)}, u32[]{:S(2)}, u32[]{:S(2)}) async-start(bf16[16,4,1024]{2,1,0:T(4,128)(2,1)} %broadcast_in_dim.48), calls=%async_computation | async-start | bytes 262144 | tf_op jit(solution)/shard_map/all_to_all | solution.py:151
  8.5 0.0 collective-permute-done.2
  8.5 0.0 copy-done.5
  8.5 6.0 %all-to-all-done = bf16[16,4,1024]{2,1,0:T(4,128)(2,1)S(1)} async-done(((bf16[16,4,1024]{2,1,0:T(4,128)(2,1)}), bf16[16,4,1024]{2,1,0:T(4,128)(2,1)S(1)}, u32[]{:S(2)}, u32[]{:S(2)}) %all-to-all-start) | async-done | bytes 131104 | tf_op jit(solution)/shard_map/all_to_all | solution.py:151
  14.5 0.7 %broadcast_in_dim.50 = bf16[8,16,1024]{2,1,0:T(8,128)(2,1)} broadcast(bf16[16,1024]{1,0:T(8,128)(2,1)S(1)} %maximum_bitcast_fusion), dimensions={1,2} | broadcast | bytes 294912 | tf_op jit(solution)/shard_map/broadcast_in_dim | solution.py:160
  15.3 7.1 %all-to-all-start.1 = ((bf16[8,16,1024]{2,1,0:T(8,128)(2,1)}), bf16[8,16,1024]{2,1,0:T(8,128)(2,1)S(1)}, u32[]{:S(2)}, u32[]{:S(2)}) async-start(bf16[8,16,1024]{2,1,0:T(8,128)(2,1)} %broadcast_in_dim.50), calls=%async_computation.1 | async-start | bytes 524288 | tf_op jit(solution)/shard_map/all_to_all | solution.py:159
  22.4 5.4 %collective-permute-start = (bf16[64,1024]{1,0:T(8,128)(2,1)S(1)}, bf16[64,1024]{1,0:T(8,128)(2,1)S(1)}, u32[]{:S(2)}, u32[]{:S(2)}) collective-permute-start(bf16[64,1024]{1,0:T(8,128)(2,1)S(1)} %reshape.61.own_ref), channel_id=1, source_target_pairs={{0,1},{1,2},{2,3},{3,4},{4,5},{5,6},{6,7},{7,8},{8,9},{9,10},{10,1... | collective-permute-start | bytes 393224 | tf_op jit(solution)/shard_map/ppermute | solution.py:164
  27.9 1.9 %collective-permute-start.1 = (bf16[64,1024]{1,0:T(8,128)(2,1)S(1)}, bf16[64,1024]{1,0:T(8,128)(2,1)S(1)}, u32[]{:S(2)}, u32[]{:S(2)}) collective-permute-start(bf16[64,1024]{1,0:T(8,128)(2,1)S(1)} %reshape.61.own_ref), channel_id=1, source_target_pairs={{1,0},{2,1},{3,2},{4,3},{5,4},{6,5},{7,6},{8,7},{9,8},{10,9},{11,1... | collective-permute-start | bytes 393224 | tf_op jit(solution)/shard_map/ppermute | solution.py:165
  29.8 0.1 broadcast_and_fusion
  29.9 0.5 collective-permute-done.low_ref
  30.3 6.9 %collective-permute-done.1.high_ref = bf16[64,1024]{1,0:T(8,128)(2,1)S(1)} collective-permute-done((bf16[64,1024]{1,0:T(8,128)(2,1)S(1)}, bf16[64,1024]{1,0:T(8,128)(2,1)S(1)}, u32[]{:S(2)}, u32[]{:S(2)}) %collective-permute-start.1) | collective-permute-done | bytes 131104 | tf_op jit(solution)/shard_map/ppermute | solution.py:165
  37.2 0.0 all-to-all-done.1
  37.2 0.0 copy-start.6
  37.2 0.0 copy-start.1
  37.2 0.0 copy-start.2
  37.2 1.0 %shard_map.82 = bf16[16,36,128]{2,1,0:T(8,128)(2,1)} custom-call(bf16[64,1024]{1,0:T(8,128)(2,1)S(1)} %collective-permute-done.low_ref, bf16[64,1024]{1,0:T(8,128)(2,1)S(1)} %reshape.61.own_ref, bf16[64,1024]{1,0:T(8,128)(2,1)S(1)} %collective-permute-done.1.high_ref, bf16[128,1024]{1,0:T(8,128)(2,1)S(1)} %bitcast.4), custom_call_target="tpu_custom_call" | custom-call | flops 67108864 | bytes 1048576 | tf_op jit(solution)/shard_map/pallas_call | solution.py:139
  38.2 0.0 copy-start
  38.2 6.0 %all-to-all-start.2 = ((bf16[16,36,128]{2,1,0:T(8,128)(2,1)}), bf16[16,36,128]{2,1,0:T(8,128)(2,1)S(1)}, u32[]{:S(2)}, u32[]{:S(2)}) async-start(bf16[16,36,128]{2,1,0:T(8,128)(2,1)} %shard_map.82), calls=%async_computation.2 | async-start | bytes 327680 | tf_op jit(solution)/shard_map/all_to_all | solution.py:197
  44.1 0.0 copy-done.6
  44.1 0.1 broadcast_select_fusion.2
  44.2 0.0 copy-start.3
  44.2 0.0 copy-start.4
  44.3 0.1 broadcast_in_dim.55
  44.3 0.0 copy-done.1
  44.4 0.0 copy-done.2
  44.4 0.0 copy-done
  44.4 0.5 %copy-done.3 = f32[8,81]{1,0:T(8,128)S(1)} copy-done((f32[8,81]{1,0:T(8,128)S(1)}, f32[8,81]{1,0:T(8,128)}, u32[]{:S(2)}) %copy-start.3) | copy-done | bytes 2616
  44.9 0.0 copy-done.4
  44.9 0.5 %shard_map.83 = (bf16[256,256]{1,0:T(8,128)(2,1)S(1)}, bf16[80,256]{1,0:T(8,128)(2,1)S(1)}) custom-call(f32[8,81]{1,0:T(8,128)S(1)} %copy-done.3, f32[8,81]{1,0:T(8,128)S(1)} %copy-done.4, bf16[81,81]{1,0:T(8,128)(2,1)S(1)} %copy-done.2, bf16[81,2048]{1,0:T(8,128)(2,1)S(1)} %copy-done, bf16[81,2048]{1,0:T(8,128)(2,1)S(1)} %copy-done.1), custom_call_target="tpu_custom_call" | custom-call | flops 16777216 | bytes 1048576 | tf_op jit(solution)/shard_map/pallas_call | solution.py:139
  45.5 5.1 %all-to-all-done.2.r_ref = bf16[16,36,128]{2,1,0:T(8,128)(2,1)S(1)} async-done(((bf16[16,36,128]{2,1,0:T(8,128)(2,1)}), bf16[16,36,128]{2,1,0:T(8,128)(2,1)S(1)}, u32[]{:S(2)}, u32[]{:S(2)}) %all-to-all-start.2) | async-done | bytes 147488 | tf_op jit(solution)/shard_map/all_to_all | solution.py:197
  50.6 0.1 broadcast_in_dim.56.bias_ref
  50.6 3.0 %shard_map.84 = f32[64,128]{1,0:T(8,128)} custom-call(bf16[16,36,128]{2,1,0:T(8,128)(2,1)S(1)} %all-to-all-done.2.r_ref, bf16[256,256]{1,0:T(8,128)(2,1)S(1)} %get-tuple-element.7.w1_ref, bf16[80,256]{1,0:T(8,128)(2,1)S(1)} %get-tuple-element.8.w2_ref, f32[256,128]{1,0:T(8,128)S(1)} %broadcast_in_dim.56.bias_ref), custom_call_target="tpu_custom_call" | custom-call | flops 268435456 | bytes 1048576 | tf_op jit(solution)/shard_map/pallas_call | solution.py:139
  (5 shorter events, 0.1 us)
Async XLA Ops:
  0.0 8.5 %collective-permute-start.2 = (bf16[1,8,1024]{2,1,0:T(8,128)(2,1)}, bf16[1,8,1024]{2,1,0:T(8,128)(2,1)S(1)}, u32[]{:S(2)}, u32[]{:S(2)}) collective-permute-start(bf16[1,8,1024]{2,1,0:T(8,128)(2,1)} %param.8), channel_id=1, source_target_pairs={{0,1},{1,0},{2,3},{3,2},{4,5},{5,4},{6,7},{7,6},{8,9},{9,8},{10,11... | collective-permute-start | bytes 49160 | tf_op jit(solution)/shard_map/ppermute | solution.py:154
  1.5 7.0 %copy-start.5 = (bf16[1,8,1024]{2,1,0:T(8,128)(2,1)S(1)}, bf16[1,8,1024]{2,1,0:T(8,128)(2,1)}, u32[]{:S(2)}) copy-start(bf16[1,8,1024]{2,1,0:T(8,128)(2,1)} %param.8) | copy-start | bytes 49156
  1.5 13.1 %all-to-all-start = ((bf16[16,4,1024]{2,1,0:T(4,128)(2,1)}), bf16[16,4,1024]{2,1,0:T(4,128)(2,1)S(1)}, u32[]{:S(2)}, u32[]{:S(2)}) async-start(bf16[16,4,1024]{2,1,0:T(4,128)(2,1)} %broadcast_in_dim.48), calls=%async_computation | async-start | bytes 262144 | tf_op jit(solution)/shard_map/all_to_all | solution.py:151
  15.3 21.9 %all-to-all-start.1 = ((bf16[8,16,1024]{2,1,0:T(8,128)(2,1)}), bf16[8,16,1024]{2,1,0:T(8,128)(2,1)S(1)}, u32[]{:S(2)}, u32[]{:S(2)}) async-start(bf16[8,16,1024]{2,1,0:T(8,128)(2,1)} %broadcast_in_dim.50), calls=%async_computation.1 | async-start | bytes 524288 | tf_op jit(solution)/shard_map/all_to_all | solution.py:159
  22.4 7.9 %collective-permute-start = (bf16[64,1024]{1,0:T(8,128)(2,1)S(1)}, bf16[64,1024]{1,0:T(8,128)(2,1)S(1)}, u32[]{:S(2)}, u32[]{:S(2)}) collective-permute-start(bf16[64,1024]{1,0:T(8,128)(2,1)S(1)} %reshape.61.own_ref), channel_id=1, source_target_pairs={{0,1},{1,2},{2,3},{3,4},{4,5},{5,6},{6,7},{7,8},{8,9},{9,10},{10,1... | collective-permute-start | bytes 393224 | tf_op jit(solution)/shard_map/ppermute | solution.py:164
  27.9 9.3 %collective-permute-start.1 = (bf16[64,1024]{1,0:T(8,128)(2,1)S(1)}, bf16[64,1024]{1,0:T(8,128)(2,1)S(1)}, u32[]{:S(2)}, u32[]{:S(2)}) collective-permute-start(bf16[64,1024]{1,0:T(8,128)(2,1)S(1)} %reshape.61.own_ref), channel_id=1, source_target_pairs={{1,0},{2,1},{3,2},{4,3},{5,4},{6,5},{7,6},{8,7},{9,8},{10,9},{11,1... | collective-permute-start | bytes 393224 | tf_op jit(solution)/shard_map/ppermute | solution.py:165
  37.2 6.9 %copy-start.6 = (f32[8]{0:T(128)S(1)}, f32[8]{0:T(128)}, u32[]{:S(2)}) copy-start(f32[8]{0:T(128)} %param.11) | copy-start | bytes 100
  37.2 7.2 %copy-start.1 = (bf16[81,2048]{1,0:T(8,128)(2,1)S(1)}, bf16[81,2048]{1,0:T(8,128)(2,1)}, u32[]{:S(2)}) copy-start(bf16[81,2048]{1,0:T(8,128)(2,1)} %constant.34.clone.sel2_ref) | copy-start | bytes 995332
  37.2 7.2 %copy-start.2 = (bf16[81,81]{1,0:T(8,128)(2,1)S(1)}, bf16[81,81]{1,0:T(8,128)(2,1)}, u32[]{:S(2)}) copy-start(bf16[81,81]{1,0:T(8,128)(2,1)} %constant.32.clone.mirror_ref) | copy-start | bytes 39370
  38.2 6.2 %copy-start = (bf16[81,2048]{1,0:T(8,128)(2,1)S(1)}, bf16[81,2048]{1,0:T(8,128)(2,1)}, u32[]{:S(2)}) copy-start(bf16[81,2048]{1,0:T(8,128)(2,1)} %constant.33.clone.sel1_ref) | copy-start | bytes 995332
  38.2 12.4 %all-to-all-start.2 = ((bf16[16,36,128]{2,1,0:T(8,128)(2,1)}), bf16[16,36,128]{2,1,0:T(8,128)(2,1)S(1)}, u32[]{:S(2)}, u32[]{:S(2)}) async-start(bf16[16,36,128]{2,1,0:T(8,128)(2,1)} %shard_map.82), calls=%async_computation.2 | async-start | bytes 327680 | tf_op jit(solution)/shard_map/all_to_all | solution.py:197
  44.2 0.7 %copy-start.3 = (f32[8,81]{1,0:T(8,128)S(1)}, f32[8,81]{1,0:T(8,128)}, u32[]{:S(2)}) copy-start(f32[8,81]{1,0:T(8,128)} %cin_ref.1) | copy-start | bytes 7780
  44.2 0.7 %copy-start.4 = (f32[8,81]{1,0:T(8,128)S(1)}, f32[8,81]{1,0:T(8,128)}, u32[]{:S(2)}) copy-start(f32[8,81]{1,0:T(8,128)} %cout_ref.1) | copy-start | bytes 7780

commit v3 on v2

--- a/solution.py
+++ b/solution.py
@@ -5,6 +5,7 @@
 from jax.experimental import pallas as pl
 from jax.experimental.pallas import tpu as pltpu
 from jax.sharding import PartitionSpec as P
+
 
 SHIFTS = (-1, 0, 1)
 
@@ -67,16 +68,39 @@
     w2_ref[...] = jnp.concatenate(rows, axis=0).astype(jnp.bfloat16)
 
 
-def volume_kernel(low_ref, own_ref, high_ref, a_ref, o_ref, scr_ref, tmp_ref):
-    tall = jnp.concatenate([low_ref[...], own_ref[...], high_ref[...]], axis=0)
+def store_copies(source, target, sems):
+    stores = [
+        pltpu.make_async_copy(source, target.at[n], sems.at[n]) for n in range(target.shape[0])
+    ]
+    for store in stores:
+        store.start()
+    for store in stores:
+        store.wait()
+
+
+def b_copies_kernel(b_ref, o_ref, out_sem):
+    store_copies(b_ref, o_ref, out_sem)
+
+
+def a_copies_kernel(mine_ref, other_ref, y_ref, o_ref, v_ref, out_sem):
+    first = y_ref[0] == 0
+    mine, other = mine_ref[...], other_ref[...]
+    v_ref[0] = jnp.where(first, mine, other)
+    v_ref[1] = jnp.where(first, other, mine)
+    store_copies(v_ref, o_ref, out_sem)
+
+
+def volume_kernel(far_ref, own_ref, near_ref, a_ref, y_ref, o_ref, scr_ref, tmp_ref):
+    tall = jnp.concatenate([far_ref[...], own_ref[...], near_ref[...]], axis=0)
     scores = lax.dot_general(
         tall, a_ref[...], (((1,), (1,)), ((), ())), preferred_element_type=jnp.float32
     ) * (1024 ** -0.5)
     zeros = jnp.zeros((8, 128), jnp.float32)
-    for n in range(3):
-        scr_ref[n, 0:8, :] = zeros
-        scr_ref[n, 8:72, :] = scores[64 * n : 64 * n + 64]
-        scr_ref[n, 72:80, :] = zeros
+    far = 2 * y_ref[0]
+    for n, slot in enumerate((far, 1, 2 - far)):
+        scr_ref[slot, 0:8, :] = zeros
+        scr_ref[slot, 8:72, :] = scores[64 * n : 64 * n + 64]
+        scr_ref[slot, 72:80, :] = zeros
     for s in range(16):
         for n in range(3):
             tmp_ref[s, 12 * n : 12 * n + 12, :] = scr_ref[n, 4 + 4 * s : 16 + 4 * s, :]
@@ -133,6 +157,8 @@
 
 
 VMEM = pl.BlockSpec(memory_space=pltpu.VMEM)
+SMEM = pl.BlockSpec(memory_space=pltpu.SMEM)
+HBM = pl.BlockSpec(memory_space=pltpu.HBM)
 
 
 def call(kernel, outs, scratch, flops, *args):
@@ -148,21 +174,36 @@
 
 
 def per_device(feature_a, feature_b, conv_in, bias_in, conv_out):
-    b = lax.all_to_all(
-        jnp.broadcast_to(feature_b.reshape(1, 4, 1024), (16, 4, 1024)), "src", 0, 0, tiled=True
-    ).reshape(64, 1024)
+    y_half = lax.axis_index("yh").reshape(1)
+    b = pl.pallas_call(
+        b_copies_kernel,
+        out_shape=jax.ShapeDtypeStruct((16, 2, 2, 1024), jnp.bfloat16),
+        in_specs=[VMEM],
+        out_specs=HBM,
+        scratch_shapes=[pltpu.SemaphoreType.DMA((16,))],
+        compiler_params=pltpu.CompilerParams(vmem_limit_bytes=16 << 20),
+    )(feature_b)
+    b = lax.all_to_all(b, "src", 0, 0, tiled=True)
+    b = b.reshape(64, 1024)
     other = lax.ppermute(feature_a, "yh", [(0, 1), (1, 0)])
-    first = lax.axis_index("yh") == 0
-    wide = jnp.concatenate(
-        [jnp.where(first, feature_a, other), jnp.where(first, other, feature_a)], axis=1
-    )
-    wide = lax.all_to_all(
-        jnp.broadcast_to(wide, (8, 16, 1024)), "z", 0, 0, tiled=True
-    ).reshape(128, 1024)
-    up = [(i, i + 1) for i in range(15)]
-    down = [(i + 1, i) for i in range(15)]
-    low = lax.ppermute(b, ("z", "yh"), up)
-    high = lax.ppermute(b, ("z", "yh"), down)
+    wide = pl.pallas_call(
+        a_copies_kernel,
+        out_shape=jax.ShapeDtypeStruct((8, 2, 8, 1024), jnp.bfloat16),
+        in_specs=[VMEM, VMEM, SMEM],
+        out_specs=HBM,
+        scratch_shapes=[
+            pltpu.VMEM((2, 8, 1024), jnp.bfloat16),
+            pltpu.SemaphoreType.DMA((8,)),
+        ],
+        compiler_params=pltpu.CompilerParams(vmem_limit_bytes=16 << 20),
+    )(feature_a[0], other[0], y_half)
+    wide = lax.all_to_all(wide, "z", 0, 0, tiled=True)
+    wide = wide.reshape(128, 1024)
+    near = [(2 * z + y, 2 * z + 1 - y) for z in range(8) for y in range(2)]
+    far = [(2 * z + 1, 2 * z + 2) for z in range(7)]
+    far += [(target, source) for source, target in far]
+    near = lax.ppermute(b, ("z", "yh"), near)
+    far = lax.ppermute(b, ("z", "yh"), far)
     w1, w2 = call(
         weights_kernel,
         (
@@ -184,16 +225,18 @@
         inside[:, :, None, None, None], bias_in[None, None, None, :, None], -1e30
     )
     bias = jnp.broadcast_to(bias, (4, 4, 2, 8, 128)).reshape(256, 128)
-    pieces = call(
+    pieces = pl.pallas_call(
         volume_kernel,
-        jax.ShapeDtypeStruct((16, 36, 128), jnp.bfloat16),
-        [pltpu.VMEM((3, 80, 128), jnp.float32), pltpu.VMEM((16, 40, 128), jnp.float32)],
-        1 << 26,
-        low,
-        b,
-        high,
-        wide,
-    )
+        out_shape=jax.ShapeDtypeStruct((16, 36, 128), jnp.bfloat16),
+        in_specs=[VMEM] * 4 + [SMEM],
+        out_specs=VMEM,
+        scratch_shapes=[
+            pltpu.VMEM((3, 80, 128), jnp.float32),
+            pltpu.VMEM((16, 40, 128), jnp.float32),
+        ],
+        compiler_params=pltpu.CompilerParams(vmem_limit_bytes=16 << 20),
+        cost_estimate=pl.CostEstimate(flops=1 << 26, bytes_accessed=1 << 20, transcendentals=0),
+    )(far, b, near, wide, y_half)
     pieces = lax.all_to_all(pieces, "src", 0, 0, tiled=True)
     out = call(
         consensus_kernel,

time: 54.2 us -> 51.5 us (0.950)
  the two profiles are of different devices: /device:TPU:113 before, /device:TPU:1 now
where the time goes in v3:
time: 51.5 us; the launch traced here: 50.8 us
  starting transfers between devices  30.2 us (59%)
  waiting for transfers between devices  12.7 us (25%)
  Pallas kernels  6.14 us (12%)
  local copies, waits for them, and re-layouts  1.52 us (3%)
    all_to_all x1, starting transfers between devices, per_device(): wide = lax.all_to_all(wide, 'z', 0, 0, tiled=True)  8.19 us
    all_to_all x1, starting transfers between devices, per_device(): b = lax.all_to_all(b, 'src', 0, 0, tiled=True)  6.83 us
    all_to_all x1, starting transfers between devices, per_device(): pieces = lax.all_to_all(pieces, 'src', 0, 0, tiled=True)  6.33 us
    ppermute x1, starting transfers between devices, per_device(): near = lax.ppermute(b, ('z', 'yh'), near)  5.47 us
    ppermute x1, waiting for transfers between devices, per_device(): near = lax.ppermute(b, ('z', 'yh'), near)  5.17 us
    all_to_all x1, waiting for transfers between devices, per_device(): pieces = lax.all_to_all(pieces, 'src', 0, 0, tiled=True)  4.99 us
    pallas_call x2, Pallas kernels, call(): pl.pallas_call(kernel, out_shape=outs, in_specs=[VMEM] * len(args), out_s...  3.58 us
    ppermute x1, starting transfers between devices, per_device(): other = lax.ppermute(feature_a, 'yh', [(0, 1), (1, 0)])  2.71 us
  transfers between devices with their start and end apart: 6, of which 4 were waited for; matrix products, arithmetic and copies ran while one was open for 1% of the time, Pallas kernels for 3%

profile of v3, /device:TPU:1, one launch (start us, length us, event | category | flops | bytes accessed | tf_op | source)
XLA Modules:
  0.0 50.8 jit_solution(3467724471751401114)
XLA Ops:
  0.0 0.0 copy-start.4
  0.0 0.7 %copy-done.4 = bf16[2,2,1024]{2,1,0:T(2,128)(2,1)S(1)} copy-done((bf16[2,2,1024]{2,1,0:T(2,128)(2,1)S(1)}, bf16[2,2,1024]{2,1,0:T(2,128)(2,1)}, u32[]{:S(2)}) %copy-start.4) | copy-done | bytes 8216
  0.7 0.8 %shard_map.82 = bf16[16,2,2,1024]{3,2,1,0:T(2,128)(2,1)} custom-call(bf16[2,2,1024]{2,1,0:T(2,128)(2,1)S(1)} %copy-done.4), custom_call_target="tpu_custom_call" | custom-call | tf_op jit(solution)/shard_map/pallas_call | solution.py:178
  1.5 0.0 copy-start.3
  1.5 6.8 %all-to-all-start = ((bf16[16,2,2,1024]{3,2,1,0:T(2,128)(2,1)}), bf16[16,2,2,1024]{3,2,1,0:T(2,128)(2,1)S(1)}, u32[]{:S(2)}, u32[]{:S(2)}) async-start(bf16[16,2,2,1024]{3,2,1,0:T(2,128)(2,1)} %shard_map.82), calls=%async_computation | async-start | bytes 262144 | tf_op jit(solution)/shard_map/all_to_all | solution.py:186
  8.3 0.0 copy-done.3
  8.4 2.7 %collective-permute-start.2 = (bf16[1,8,1024]{2,1,0:T(8,128)(2,1)S(1)}, bf16[1,8,1024]{2,1,0:T(8,128)(2,1)S(1)}, u32[]{:S(2)}, u32[]{:S(2)}) collective-permute-start(bf16[1,8,1024]{2,1,0:T(8,128)(2,1)S(1)} %copy-done.3), channel_id=1, source_target_pairs={{0,1},{1,0},{2,3},{3,2},{4,5},{5,4},{6,7},{7,6},{8,9},{9,8},{10,11... | collective-permute-start | bytes 49160 | tf_op jit(solution)/shard_map/ppermute | solution.py:188
  11.1 1.6 %collective-permute-done.2 = bf16[1,8,1024]{2,1,0:T(8,128)(2,1)S(1)} collective-permute-done((bf16[1,8,1024]{2,1,0:T(8,128)(2,1)S(1)}, bf16[1,8,1024]{2,1,0:T(8,128)(2,1)S(1)}, u32[]{:S(2)}, u32[]{:S(2)}) %collective-permute-start.2) | collective-permute-done | bytes 16416 | tf_op jit(solution)/shard_map/ppermute | solution.py:188
  12.7 0.8 %shard_map.83 = bf16[8,2,8,1024]{3,2,1,0:T(8,128)(2,1)} custom-call(bf16[8,1024]{1,0:T(8,128)(2,1)S(1)} %bitcast.6, bf16[8,1024]{1,0:T(8,128)(2,1)S(1)} %bitcast.7, s32[1]{0:T(128)} %bitcast.2.y_ref), custom_call_target="tpu_custom_call" | custom-call | tf_op jit(solution)/shard_map/pallas_call | solution.py:189
  13.4 0.9 %all-to-all-done = bf16[16,2,2,1024]{3,2,1,0:T(2,128)(2,1)S(1)} async-done(((bf16[16,2,2,1024]{3,2,1,0:T(2,128)(2,1)}), bf16[16,2,2,1024]{3,2,1,0:T(2,128)(2,1)S(1)}, u32[]{:S(2)}, u32[]{:S(2)}) %all-to-all-start) | async-done | bytes 131104 | tf_op jit(solution)/shard_map/all_to_all | solution.py:186
  14.4 8.2 %all-to-all-start.1 = ((bf16[8,2,8,1024]{3,2,1,0:T(8,128)(2,1)}), bf16[8,2,8,1024]{3,2,1,0:T(8,128)(2,1)S(1)}, u32[]{:S(2)}, u32[]{:S(2)}) async-start(bf16[8,2,8,1024]{3,2,1,0:T(8,128)(2,1)} %shard_map.83), calls=%async_computation.1 | async-start | bytes 524288 | tf_op jit(solution)/shard_map/all_to_all | solution.py:200
  22.6 0.1 reshape.62.own_ref
  22.7 0.7 %collective-permute-start = (bf16[64,1024]{1,0:T(8,128)(2,1)S(1)}, bf16[64,1024]{1,0:T(8,128)(2,1)S(1)}, u32[]{:S(2)}, u32[]{:S(2)}) collective-permute-start(bf16[64,1024]{1,0:T(8,128)(2,1)S(1)} %reshape.62.own_ref), channel_id=1, source_target_pairs={{1,2},{3,4},{5,6},{7,8},{9,10},{11,12},{13,14},{2,1},{4,3},{6,5},{... | collective-permute-start | bytes 393224 | tf_op jit(solution)/shard_map/ppermute | solution.py:206
  23.3 5.5 %collective-permute-start.1 = (bf16[64,1024]{1,0:T(8,128)(2,1)S(1)}, bf16[64,1024]{1,0:T(8,128)(2,1)S(1)}, u32[]{:S(2)}, u32[]{:S(2)}) collective-permute-start(bf16[64,1024]{1,0:T(8,128)(2,1)S(1)} %reshape.62.own_ref), channel_id=1, source_target_pairs={{0,1},{1,0},{2,3},{3,2},{4,5},{5,4},{6,7},{7,6},{8,9},{9,8},{10,11... | collective-permute-start | bytes 393224 | tf_op jit(solution)/shard_map/ppermute | solution.py:205
  28.8 0.1 broadcast_and_fusion
  28.9 0.0 collective-permute-done.far_ref
  28.9 5.2 %collective-permute-done.1.near_ref = bf16[64,1024]{1,0:T(8,128)(2,1)S(1)} collective-permute-done((bf16[64,1024]{1,0:T(8,128)(2,1)S(1)}, bf16[64,1024]{1,0:T(8,128)(2,1)S(1)}, u32[]{:S(2)}, u32[]{:S(2)}) %collective-permute-start.1) | collective-permute-done | bytes 131104 | tf_op jit(solution)/shard_map/ppermute | solution.py:205
  34.0 0.0 all-to-all-done.1
  34.1 0.0 copy-start.7
  34.1 0.0 copy-start.1
  34.1 0.0 copy-start.2
  34.1 1.0 %shard_map.84 = bf16[16,36,128]{2,1,0:T(8,128)(2,1)} custom-call(bf16[64,1024]{1,0:T(8,128)(2,1)S(1)} %collective-permute-done.far_ref, bf16[64,1024]{1,0:T(8,128)(2,1)S(1)} %reshape.62.own_ref, bf16[64,1024]{1,0:T(8,128)(2,1)S(1)} %collective-permute-done.1.near_ref, bf16[128,1024]{1,0:T(8,128)(2,1)S(1)} %bitcast.5, s32[1]{0:T(128)} %bitcast.2.y_ref), custom_call_target="tpu_custom_call" | custom-call | flops 67108864 | bytes 1048576 | tf_op jit(solution)/shard_map/pallas_call | solution.py:228
  35.0 0.0 copy-start
  35.0 6.3 %all-to-all-start.2 = ((bf16[16,36,128]{2,1,0:T(8,128)(2,1)}), bf16[16,36,128]{2,1,0:T(8,128)(2,1)S(1)}, u32[]{:S(2)}, u32[]{:S(2)}) async-start(bf16[16,36,128]{2,1,0:T(8,128)(2,1)} %shard_map.84), calls=%async_computation.2 | async-start | bytes 327680 | tf_op jit(solution)/shard_map/all_to_all | solution.py:240
  41.4 0.0 copy-done.7
  41.4 0.1 broadcast_select_fusion
  41.5 0.0 copy-start.5
  41.5 0.0 copy-start.6
  41.5 0.1 broadcast_in_dim.37
  41.6 0.0 copy-done.1
  41.6 0.0 copy-done.2
  41.6 0.0 copy-done
  41.6 0.5 %copy-done.5 = f32[8,81]{1,0:T(8,128)S(1)} copy-done((f32[8,81]{1,0:T(8,128)S(1)}, f32[8,81]{1,0:T(8,128)}, u32[]{:S(2)}) %copy-start.5) | copy-done | bytes 2616
  42.2 0.0 copy-done.6
  42.2 0.5 %shard_map.85 = (bf16[256,256]{1,0:T(8,128)(2,1)S(1)}, bf16[80,256]{1,0:T(8,128)(2,1)S(1)}) custom-call(f32[8,81]{1,0:T(8,128)S(1)} %copy-done.5, f32[8,81]{1,0:T(8,128)S(1)} %copy-done.6, bf16[81,81]{1,0:T(8,128)(2,1)S(1)} %copy-done.2, bf16[81,2048]{1,0:T(8,128)(2,1)S(1)} %copy-done, bf16[81,2048]{1,0:T(8,128)(2,1)S(1)} %copy-done.1), custom_call_target="tpu_custom_call" | custom-call | flops 16777216 | bytes 1048576 | tf_op jit(solution)/shard_map/pallas_call | solution.py:165
  42.7 5.0 %all-to-all-done.2.r_ref = bf16[16,36,128]{2,1,0:T(8,128)(2,1)S(1)} async-done(((bf16[16,36,128]{2,1,0:T(8,128)(2,1)}), bf16[16,36,128]{2,1,0:T(8,128)(2,1)S(1)}, u32[]{:S(2)}, u32[]{:S(2)}) %all-to-all-start.2) | async-done | bytes 147488 | tf_op jit(solution)/shard_map/all_to_all | solution.py:240
  47.7 0.1 broadcast_in_dim.38.bias_ref
  47.8 3.0 %shard_map.86 = f32[64,128]{1,0:T(8,128)} custom-call(bf16[16,36,128]{2,1,0:T(8,128)(2,1)S(1)} %all-to-all-done.2.r_ref, bf16[256,256]{1,0:T(8,128)(2,1)S(1)} %get-tuple-element.7.w1_ref, bf16[80,256]{1,0:T(8,128)(2,1)S(1)} %get-tuple-element.8.w2_ref, f32[256,128]{1,0:T(8,128)S(1)} %broadcast_in_dim.38.bias_ref), custom_call_target="tpu_custom_call" | custom-call | flops 268435456 | bytes 1048576 | tf_op jit(solution)/shard_map/pallas_call | solution.py:165
  (2 shorter events, 0.0 us)
Async XLA Ops:
  0.0 0.7 %copy-start.4 = (bf16[2,2,1024]{2,1,0:T(2,128)(2,1)S(1)}, bf16[2,2,1024]{2,1,0:T(2,128)(2,1)}, u32[]{:S(2)}) copy-start(bf16[2,2,1024]{2,1,0:T(2,128)(2,1)} %b_ref.1) | copy-start | bytes 24580
  1.5 6.8 %copy-start.3 = (bf16[1,8,1024]{2,1,0:T(8,128)(2,1)S(1)}, bf16[1,8,1024]{2,1,0:T(8,128)(2,1)}, u32[]{:S(2)}) copy-start(bf16[1,8,1024]{2,1,0:T(8,128)(2,1)} %param.8) | copy-start | bytes 49156
  1.5 12.9 %all-to-all-start = ((bf16[16,2,2,1024]{3,2,1,0:T(2,128)(2,1)}), bf16[16,2,2,1024]{3,2,1,0:T(2,128)(2,1)S(1)}, u32[]{:S(2)}, u32[]{:S(2)}) async-start(bf16[16,2,2,1024]{3,2,1,0:T(2,128)(2,1)} %shard_map.82), calls=%async_computation | async-start | bytes 262144 | tf_op jit(solution)/shard_map/all_to_all | solution.py:186
  8.4 4.3 %collective-permute-start.2 = (bf16[1,8,1024]{2,1,0:T(8,128)(2,1)S(1)}, bf16[1,8,1024]{2,1,0:T(8,128)(2,1)S(1)}, u32[]{:S(2)}, u32[]{:S(2)}) collective-permute-start(bf16[1,8,1024]{2,1,0:T(8,128)(2,1)S(1)} %copy-done.3), channel_id=1, source_target_pairs={{0,1},{1,0},{2,3},{3,2},{4,5},{5,4},{6,7},{7,6},{8,9},{9,8},{10,11... | collective-permute-start | bytes 49160 | tf_op jit(solution)/shard_map/ppermute | solution.py:188
  14.4 19.7 %all-to-all-start.1 = ((bf16[8,2,8,1024]{3,2,1,0:T(8,128)(2,1)}), bf16[8,2,8,1024]{3,2,1,0:T(8,128)(2,1)S(1)}, u32[]{:S(2)}, u32[]{:S(2)}) async-start(bf16[8,2,8,1024]{3,2,1,0:T(8,128)(2,1)} %shard_map.83), calls=%async_computation.1 | async-start | bytes 524288 | tf_op jit(solution)/shard_map/all_to_all | solution.py:200
  22.7 6.2 %collective-permute-start = (bf16[64,1024]{1,0:T(8,128)(2,1)S(1)}, bf16[64,1024]{1,0:T(8,128)(2,1)S(1)}, u32[]{:S(2)}, u32[]{:S(2)}) collective-permute-start(bf16[64,1024]{1,0:T(8,128)(2,1)S(1)} %reshape.62.own_ref), channel_id=1, source_target_pairs={{1,2},{3,4},{5,6},{7,8},{9,10},{11,12},{13,14},{2,1},{4,3},{6,5},{... | collective-permute-start | bytes 393224 | tf_op jit(solution)/shard_map/ppermute | solution.py:206
  23.3 10.7 %collective-permute-start.1 = (bf16[64,1024]{1,0:T(8,128)(2,1)S(1)}, bf16[64,1024]{1,0:T(8,128)(2,1)S(1)}, u32[]{:S(2)}, u32[]{:S(2)}) collective-permute-start(bf16[64,1024]{1,0:T(8,128)(2,1)S(1)} %reshape.62.own_ref), channel_id=1, source_target_pairs={{0,1},{1,0},{2,3},{3,2},{4,5},{5,4},{6,7},{7,6},{8,9},{9,8},{10,11... | collective-permute-start | bytes 393224 | tf_op jit(solution)/shard_map/ppermute | solution.py:205
  34.1 7.3 %copy-start.7 = (f32[8]{0:T(128)S(1)}, f32[8]{0:T(128)}, u32[]{:S(2)}) copy-start(f32[8]{0:T(128)} %param.11) | copy-start | bytes 100
  34.1 7.5 %copy-start.1 = (bf16[81,2048]{1,0:T(8,128)(2,1)S(1)}, bf16[81,2048]{1,0:T(8,128)(2,1)}, u32[]{:S(2)}) copy-start(bf16[81,2048]{1,0:T(8,128)(2,1)} %constant.33.clone.sel2_ref) | copy-start | bytes 995332
  34.1 7.5 %copy-start.2 = (bf16[81,81]{1,0:T(8,128)(2,1)S(1)}, bf16[81,81]{1,0:T(8,128)(2,1)}, u32[]{:S(2)}) copy-start(bf16[81,81]{1,0:T(8,128)(2,1)} %constant.31.clone.mirror_ref) | copy-start | bytes 39370
  35.0 6.6 %copy-start = (bf16[81,2048]{1,0:T(8,128)(2,1)S(1)}, bf16[81,2048]{1,0:T(8,128)(2,1)}, u32[]{:S(2)}) copy-start(bf16[81,2048]{1,0:T(8,128)(2,1)} %constant.32.clone.sel1_ref) | copy-start | bytes 995332
  35.0 12.7 %all-to-all-start.2 = ((bf16[16,36,128]{2,1,0:T(8,128)(2,1)}), bf16[16,36,128]{2,1,0:T(8,128)(2,1)S(1)}, u32[]{:S(2)}, u32[]{:S(2)}) async-start(bf16[16,36,128]{2,1,0:T(8,128)(2,1)} %shard_map.84), calls=%async_computation.2 | async-start | bytes 327680 | tf_op jit(solution)/shard_map/all_to_all | solution.py:240
  41.5 0.7 %copy-start.5 = (f32[8,81]{1,0:T(8,128)S(1)}, f32[8,81]{1,0:T(8,128)}, u32[]{:S(2)}) copy-start(f32[8,81]{1,0:T(8,128)} %cin_ref.1) | copy-start | bytes 7780
  41.5 0.7 %copy-start.6 = (f32[8,81]{1,0:T(8,128)S(1)}, f32[8,81]{1,0:T(8,128)}, u32[]{:S(2)}) copy-start(f32[8,81]{1,0:T(8,128)} %cout_ref.1) | copy-start | bytes 7780

commit v4 on v3

--- a/solution.py
+++ b/solution.py
@@ -21,7 +21,7 @@
     out = np.zeros((81, 2, 4, 256), np.float32)
     for k2, l, p, q, r, s in np.ndindex(2, 4, 3, 3, 3, 3):
         k, c = k2 + p, l + q
-        column = (s * 3 + r) * 24 + k // 2 * 12 + c // 2 * 4 + k % 2 * 2 + c % 2
+        column = r * 80 + s * 24 + k // 2 * 12 + c // 2 * 4 + k % 2 * 2 + c % 2
         out[27 * p + 9 * q + 3 * r + s, k2, l, column] = 1
     return out.reshape(81, 2048)
 
@@ -41,7 +41,9 @@
     return jnp.where(lane == (127 if s == 1 else 0), 0.0, rolled)
 
 
-def weights_kernel(cin_ref, cout_ref, mirror_ref, sel1_ref, sel2_ref, w1_ref, w2_ref):
+def weights_kernel(
+    cin_ref, cout_ref, mirror_ref, sel1_ref, sel2_ref, bias_ref, at_ref, w1_ref, w2_ref
+):
     def parts(x):
         high = x.astype(jnp.bfloat16)
         low = (x - high.astype(jnp.float32)).astype(jnp.bfloat16)
@@ -52,12 +54,20 @@
         return jnp.concatenate(rows, axis=0).astype(jnp.bfloat16)
 
     t1 = jnp.dot(parts(cin_ref[...]), sel1_ref[...], preferred_element_type=jnp.float32)
-    for hl in range(2):
+    lane = lax.broadcasted_iota(jnp.int32, (16, 256), 1)
+    bias = bias_ref[...]
+    high = bias.astype(jnp.bfloat16).astype(jnp.float32)
+    for hl, part in enumerate((high, bias - high)):
         for kl in range(8):
+            block = t1[hl * 16 : hl * 16 + 16, kl * 256 : kl * 256 + 256]
+            for half in range(2):
+                row, column = at_ref[0] + half * 2 + kl // 4, at_ref[1] + kl % 4
+                inside = (row >= 0) & (row < 32) & (column >= 0) & (column < 32)
+                block = jnp.where(
+                    lane == 152 + half, jnp.where(inside, part, -1e30 if hl == 0 else 0.0), block
+                )
             row = hl * 128 + kl * 16
-            w1_ref[row : row + 16, :] = t1[
-                hl * 16 : hl * 16 + 16, kl * 256 : kl * 256 + 256
-            ].astype(jnp.bfloat16)
+            w1_ref[row : row + 16, :] = block.astype(jnp.bfloat16)
     t2 = jnp.dot(parts(cout_ref[...]), sel2_ref[...], preferred_element_type=jnp.float32)
     rows = []
     for hl in range(2):
@@ -107,34 +117,23 @@
         o_ref[s] = tmp_ref[s, 0:36, :].astype(jnp.bfloat16)
 
 
-def consensus_kernel(r_ref, w1_ref, w2_ref, bias_ref, o_ref, rf_ref, xs_ref, ps_ref):
-    zero_rows = jnp.zeros((24, 256), jnp.float32)
-    for n in range(3):
-        xs_ref[n, 0] = zero_rows
-        xs_ref[n, 17] = zero_rows
+def consensus_kernel(r_ref, w1_ref, w2_ref, o_ref, rf_ref, xs_ref, ps_ref):
+    xs_ref[0:80, :] = jnp.zeros((80, 256), jnp.bfloat16)
+    xs_ref[1360:1456, :] = jnp.zeros((96, 256), jnp.bfloat16)
+    sublane = lax.broadcasted_iota(jnp.int32, (8, 128), 0)
     for i in range(16):
         rf_ref[i] = r_ref[i].astype(jnp.float32)
         for half in range(2):
-            for d in range(0, 24, 8):
-                rows = rf_ref[i, pl.ds(half * 12 + d, 8), :]
-                for n, s in enumerate(SHIFTS):
-                    xs_ref[n, i + 1, d : d + 8, half * 128 : half * 128 + 128] = shifted(rows, s)
+            rows = [rf_ref[i, pl.ds(half * 12 + d, 8), :] for d in range(0, 24, 8)]
+            rows = [shifted(x, s) for s in SHIFTS for x in rows]
+            rows.append(jnp.where(sublane == half, 1.0, 0.0))
+            xs_ref[80 * (i + 1) : 80 * (i + 2), half * 128 : half * 128 + 128] = jnp.concatenate(
+                rows, axis=0
+            ).astype(jnp.bfloat16)
     ps_ref[0:40, :] = jnp.zeros((40, 128), jnp.float32)
     ps_ref[680:720, :] = jnp.zeros((40, 128), jnp.float32)
-    pad = jnp.zeros((40, 256), jnp.float32)
-    for i in range(0, 16, 2):
-        highs, lows = [], []
-        for d in range(2):
-            rhs = jnp.concatenate(
-                [xs_ref[n, i + d + r] for n in range(3) for r in range(3)] + [pad], axis=0
-            ).astype(jnp.bfloat16)
-            acc = jnp.dot(w1_ref[...], rhs, preferred_element_type=jnp.float32)
-            acc = acc[:128] + acc[128:]
-            hidden = jnp.concatenate([acc[:, :128], acc[:, 128:]], axis=0)
-            hidden = jnp.maximum(hidden + bias_ref[...], 0.0)
-            high = hidden.astype(jnp.bfloat16)
-            highs.append(high)
-            lows.append((hidden - high.astype(jnp.float32)).astype(jnp.bfloat16))
+
+    def second(i, highs, lows):
         both = jnp.dot(
             w2_ref[...], jnp.concatenate(highs, axis=1), preferred_element_type=jnp.float32
         )
@@ -144,6 +143,24 @@
         total = both[:40] + both[40:] + more
         ps_ref[40 * (i + 1) : 40 * (i + 2), :] = total[:, :128]
         ps_ref[40 * (i + 2) : 40 * (i + 3), :] = total[:, 128:]
+
+    def first(i):
+        rhs = xs_ref[80 * i : 80 * i + 256, :]
+        return jnp.dot(w1_ref[...], rhs, preferred_element_type=jnp.float32)
+
+    def split(acc):
+        acc = acc[:128] + acc[128:]
+        hidden = jnp.maximum(jnp.concatenate([acc[:, :128], acc[:, 128:]], axis=0), 0.0)
+        high = hidden.astype(jnp.bfloat16)
+        return high, (hidden - high.astype(jnp.float32)).astype(jnp.bfloat16)
+
+    done = None
+    for i in range(0, 16, 2):
+        sums = [first(i), first(i + 1)]
+        if done is not None:
+            second(i - 2, *done)
+        done = tuple(zip(*[split(x) for x in sums]))
+    second(14, *done)
     for kl in range(4):
         out = None
         for n, s in enumerate(SHIFTS):
@@ -204,27 +221,28 @@
     far += [(target, source) for source, target in far]
     near = lax.ppermute(b, ("z", "yh"), near)
     far = lax.ppermute(b, ("z", "yh"), far)
-    w1, w2 = call(
+    at = jnp.stack([lax.axis_index(("z", "yh")) * 2 - 1, lax.axis_index("src") * 2 - 1])
+    w1, w2 = pl.pallas_call(
         weights_kernel,
-        (
+        out_shape=(
             jax.ShapeDtypeStruct((256, 256), jnp.bfloat16),
             jax.ShapeDtypeStruct((80, 256), jnp.bfloat16),
         ),
-        [],
-        1 << 24,
+        in_specs=[VMEM] * 6 + [SMEM],
+        out_specs=(VMEM,) * 2,
+        compiler_params=pltpu.CompilerParams(vmem_limit_bytes=16 << 20),
+        cost_estimate=pl.CostEstimate(
+            flops=1 << 24, bytes_accessed=1 << 20, transcendentals=0
+        ),
+    )(
         conv_in,
         conv_out,
         jnp.asarray(mirror_matrix(), jnp.bfloat16),
         jnp.asarray(spread_in(), jnp.bfloat16),
         jnp.asarray(spread_out(), jnp.bfloat16),
+        jnp.broadcast_to(bias_in[None, :, None], (2, 8, 256)).reshape(16, 256),
+        at,
     )
-    row = lax.axis_index(("z", "yh")) * 2 - 1 + jnp.arange(4)
-    column = lax.axis_index("src") * 2 - 1 + jnp.arange(4)
-    inside = ((row >= 0) & (row < 32))[:, None] & ((column >= 0) & (column < 32))[None, :]
-    bias = jnp.where(
-        inside[:, :, None, None, None], bias_in[None, None, None, :, None], -1e30
-    )
-    bias = jnp.broadcast_to(bias, (4, 4, 2, 8, 128)).reshape(256, 128)
     pieces = pl.pallas_call(
         volume_kernel,
         out_shape=jax.ShapeDtypeStruct((16, 36, 128), jnp.bfloat16),
@@ -243,14 +261,13 @@
         jax.ShapeDtypeStruct((64, 128), jnp.float32),
         [
             pltpu.VMEM((16, 36, 128), jnp.float32),
-            pltpu.VMEM((3, 18, 24, 256), jnp.float32),
+            pltpu.VMEM((1456, 256), jnp.bfloat16),
             pltpu.VMEM((720, 128), jnp.float32),
         ],
         1 << 28,
         pieces,
         w1,
         w2,
-        bias,
     )
     return out.reshape(2, 2, 16, 128)
 

time: 51.5 us -> 50.5 us (0.981)
    pallas_call x2 -> x1, Pallas kernels: 3.58 us -> 2.19 us  [call(): pl.pallas_call(kernel, out_shape=outs, in_specs=[VMEM] * len(args), out_s...]
    pallas_call x0 -> x1, Pallas kernels: none -> 1.08 us  [per_device(): pl.pallas_call(weights_kernel, out_shape=(jax.ShapeDtypeStruct((256, 256)...]
    all_to_all x1, waiting for transfers between devices: 4.99 us -> 4.37 us  [per_device(): pieces = lax.all_to_all(pieces, 'src', 0, 0, tiled=True)]
  transfers between devices with their start and end apart: 6 -> 6, of which waited for: 4 -> 4; matrix products, arithmetic and copies ran while one was open for 1% -> 1% of each run, Pallas kernels for 3% -> 4%
where the time goes in v4:
time: 50.5 us; the launch traced here: 49.9 us
  starting transfers between devices  30.2 us (60%)
  waiting for transfers between devices  12.2 us (24%)
  Pallas kernels  5.83 us (12%)
  local copies, waits for them, and re-layouts  1.54 us (3%)
    all_to_all x1, starting transfers between devices, per_device(): wide = lax.all_to_all(wide, 'z', 0, 0, tiled=True)  8.19 us
    all_to_all x1, starting transfers between devices, per_device(): b = lax.all_to_all(b, 'src', 0, 0, tiled=True)  6.83 us
    all_to_all x1, starting transfers between devices, per_device(): pieces = lax.all_to_all(pieces, 'src', 0, 0, tiled=True)  6.35 us
    ppermute x1, starting transfers between devices, per_device(): near = lax.ppermute(b, ('z', 'yh'), near)  5.47 us
    ppermute x1, waiting for transfers between devices, per_device(): near = lax.ppermute(b, ('z', 'yh'), near)  5.22 us
    all_to_all x1, waiting for transfers between devices, per_device(): pieces = lax.all_to_all(pieces, 'src', 0, 0, tiled=True)  4.37 us
    ppermute x1, starting transfers between devices, per_device(): other = lax.ppermute(feature_a, 'yh', [(0, 1), (1, 0)])  2.71 us
    pallas_call x1, Pallas kernels, call(): pl.pallas_call(kernel, out_shape=outs, in_specs=[VMEM] * len(args), out_s...  2.19 us
  transfers between devices with their start and end apart: 6, of which 4 were waited for; matrix products, arithmetic and copies ran while one was open for 1% of the time, Pallas kernels for 4%

profile of v4, /device:TPU:1, one launch (start us, length us, event | category | flops | bytes accessed | tf_op | source)
XLA Modules:
  0.0 49.9 jit_solution(1431470931124043944)
XLA Ops:
  0.0 0.0 copy-start.4
  0.0 0.7 %copy-done.4 = bf16[2,2,1024]{2,1,0:T(2,128)(2,1)S(1)} copy-done((bf16[2,2,1024]{2,1,0:T(2,128)(2,1)S(1)}, bf16[2,2,1024]{2,1,0:T(2,128)(2,1)}, u32[]{:S(2)}) %copy-start.4) | copy-done | bytes 8216
  0.7 0.8 %shard_map.82 = bf16[16,2,2,1024]{3,2,1,0:T(2,128)(2,1)} custom-call(bf16[2,2,1024]{2,1,0:T(2,128)(2,1)S(1)} %copy-done.4), custom_call_target="tpu_custom_call" | custom-call | tf_op jit(solution)/shard_map/pallas_call | solution.py:195
  1.5 0.0 copy-start.3
  1.5 6.8 %all-to-all-start = ((bf16[16,2,2,1024]{3,2,1,0:T(2,128)(2,1)}), bf16[16,2,2,1024]{3,2,1,0:T(2,128)(2,1)S(1)}, u32[]{:S(2)}, u32[]{:S(2)}) async-start(bf16[16,2,2,1024]{3,2,1,0:T(2,128)(2,1)} %shard_map.82), calls=%async_computation | async-start | bytes 262144 | tf_op jit(solution)/shard_map/all_to_all | solution.py:203
  8.3 0.0 copy-done.3
  8.4 2.7 %collective-permute-start.2 = (bf16[1,8,1024]{2,1,0:T(8,128)(2,1)S(1)}, bf16[1,8,1024]{2,1,0:T(8,128)(2,1)S(1)}, u32[]{:S(2)}, u32[]{:S(2)}) collective-permute-start(bf16[1,8,1024]{2,1,0:T(8,128)(2,1)S(1)} %copy-done.3), channel_id=1, source_target_pairs={{0,1},{1,0},{2,3},{3,2},{4,5},{5,4},{6,7},{7,6},{8,9},{9,8},{10,11... | collective-permute-start | bytes 49160 | tf_op jit(solution)/shard_map/ppermute | solution.py:205
  11.1 1.6 %collective-permute-done.2 = bf16[1,8,1024]{2,1,0:T(8,128)(2,1)S(1)} collective-permute-done((bf16[1,8,1024]{2,1,0:T(8,128)(2,1)S(1)}, bf16[1,8,1024]{2,1,0:T(8,128)(2,1)S(1)}, u32[]{:S(2)}, u32[]{:S(2)}) %collective-permute-start.2) | collective-permute-done | bytes 16416 | tf_op jit(solution)/shard_map/ppermute | solution.py:205
  12.7 0.8 %shard_map.83 = bf16[8,2,8,1024]{3,2,1,0:T(8,128)(2,1)} custom-call(bf16[8,1024]{1,0:T(8,128)(2,1)S(1)} %bitcast.8, bf16[8,1024]{1,0:T(8,128)(2,1)S(1)} %bitcast.9, s32[1]{0:T(128)} %bitcast.2.y_ref), custom_call_target="tpu_custom_call" | custom-call | tf_op jit(solution)/shard_map/pallas_call | solution.py:206
  13.4 1.0 %all-to-all-done = bf16[16,2,2,1024]{3,2,1,0:T(2,128)(2,1)S(1)} async-done(((bf16[16,2,2,1024]{3,2,1,0:T(2,128)(2,1)}), bf16[16,2,2,1024]{3,2,1,0:T(2,128)(2,1)S(1)}, u32[]{:S(2)}, u32[]{:S(2)}) %all-to-all-start) | async-done | bytes 131104 | tf_op jit(solution)/shard_map/all_to_all | solution.py:203
  14.4 8.2 %all-to-all-start.1 = ((bf16[8,2,8,1024]{3,2,1,0:T(8,128)(2,1)}), bf16[8,2,8,1024]{3,2,1,0:T(8,128)(2,1)S(1)}, u32[]{:S(2)}, u32[]{:S(2)}) async-start(bf16[8,2,8,1024]{3,2,1,0:T(8,128)(2,1)} %shard_map.83), calls=%async_computation.1 | async-start | bytes 524288 | tf_op jit(solution)/shard_map/all_to_all | solution.py:217
  22.6 0.1 reshape.15.own_ref
  22.6 0.7 %collective-permute-start = (bf16[64,1024]{1,0:T(8,128)(2,1)S(1)}, bf16[64,1024]{1,0:T(8,128)(2,1)S(1)}, u32[]{:S(2)}, u32[]{:S(2)}) collective-permute-start(bf16[64,1024]{1,0:T(8,128)(2,1)S(1)} %reshape.15.own_ref), channel_id=1, source_target_pairs={{1,2},{3,4},{5,6},{7,8},{9,10},{11,12},{13,14},{2,1},{4,3},{6,5},{... | collective-permute-start | bytes 393224 | tf_op jit(solution)/shard_map/ppermute | solution.py:223
  23.3 5.5 %collective-permute-start.1 = (bf16[64,1024]{1,0:T(8,128)(2,1)S(1)}, bf16[64,1024]{1,0:T(8,128)(2,1)S(1)}, u32[]{:S(2)}, u32[]{:S(2)}) collective-permute-start(bf16[64,1024]{1,0:T(8,128)(2,1)S(1)} %reshape.15.own_ref), channel_id=1, source_target_pairs={{0,1},{1,0},{2,3},{3,2},{4,5},{5,4},{6,7},{7,6},{8,9},{9,8},{10,11... | collective-permute-start | bytes 393224 | tf_op jit(solution)/shard_map/ppermute | solution.py:222
  28.8 0.0 collective-permute-done.far_ref
  28.8 5.2 %collective-permute-done.1.near_ref = bf16[64,1024]{1,0:T(8,128)(2,1)S(1)} collective-permute-done((bf16[64,1024]{1,0:T(8,128)(2,1)S(1)}, bf16[64,1024]{1,0:T(8,128)(2,1)S(1)}, u32[]{:S(2)}, u32[]{:S(2)}) %collective-permute-start.1) | collective-permute-done | bytes 131104 | tf_op jit(solution)/shard_map/ppermute | solution.py:222
  34.0 0.0 all-to-all-done.1
  34.0 0.0 copy-start.7
  34.0 0.0 copy-start.1
  34.0 0.0 copy-start.2
  34.0 1.0 %shard_map.84 = bf16[16,36,128]{2,1,0:T(8,128)(2,1)} custom-call(bf16[64,1024]{1,0:T(8,128)(2,1)S(1)} %collective-permute-done.far_ref, bf16[64,1024]{1,0:T(8,128)(2,1)S(1)} %reshape.15.own_ref, bf16[64,1024]{1,0:T(8,128)(2,1)S(1)} %collective-permute-done.1.near_ref, bf16[128,1024]{1,0:T(8,128)(2,1)S(1)} %bitcast.7, s32[1]{0:T(128)} %bitcast.2.y_ref), custom_call_target="tpu_custom_call" | custom-call | flops 67108864 | bytes 1048576 | tf_op jit(solution)/shard_map/pallas_call | solution.py:246
  35.0 0.0 copy-start
  35.0 6.3 %all-to-all-start.2 = ((bf16[16,36,128]{2,1,0:T(8,128)(2,1)}), bf16[16,36,128]{2,1,0:T(8,128)(2,1)S(1)}, u32[]{:S(2)}, u32[]{:S(2)}) async-start(bf16[16,36,128]{2,1,0:T(8,128)(2,1)} %shard_map.84), calls=%async_computation.2 | async-start | bytes 327680 | tf_op jit(solution)/shard_map/all_to_all | solution.py:258
  41.4 0.0 copy-done.7
  41.4 0.1 broadcast_in_dim.11
  41.5 0.1 pad_add_fusion.at_ref
  41.5 0.0 copy-start.5
  41.5 0.0 copy-start.6
  41.5 0.1 broadcast_in_dim.12.bias_ref
  41.6 0.0 copy-done.1
  41.6 0.0 copy-done.2
  41.6 0.0 copy-done
  41.6 0.6 %copy-done.5 = f32[8,81]{1,0:T(8,128)S(1)} copy-done((f32[8,81]{1,0:T(8,128)S(1)}, f32[8,81]{1,0:T(8,128)}, u32[]{:S(2)}) %copy-start.5) | copy-done | bytes 2616
  42.2 0.0 copy-done.6
  42.2 1.1 %shard_map.85 = (bf16[256,256]{1,0:T(8,128)(2,1)S(1)}, bf16[80,256]{1,0:T(8,128)(2,1)S(1)}) custom-call(f32[8,81]{1,0:T(8,128)S(1)} %copy-done.5, f32[8,81]{1,0:T(8,128)S(1)} %copy-done.6, bf16[81,81]{1,0:T(8,128)(2,1)S(1)} %copy-done.2, bf16[81,2048]{1,0:T(8,128)(2,1)S(1)} %copy-done, bf16[81,2048]{1,0:T(8,128)(2,1)S(1)} %copy-done.1, ...), custom_call_target="tpu_custom_call" | custom-call | flops 16777216 | bytes 1048576 | tf_op jit(solution)/shard_map/pallas_call | solution.py:225
  43.3 4.4 %all-to-all-done.2.r_ref = bf16[16,36,128]{2,1,0:T(8,128)(2,1)S(1)} async-done(((bf16[16,36,128]{2,1,0:T(8,128)(2,1)}), bf16[16,36,128]{2,1,0:T(8,128)(2,1)S(1)}, u32[]{:S(2)}, u32[]{:S(2)}) %all-to-all-start.2) | async-done | bytes 147488 | tf_op jit(solution)/shard_map/all_to_all | solution.py:258
  47.7 2.2 %shard_map.86 = f32[64,128]{1,0:T(8,128)} custom-call(bf16[16,36,128]{2,1,0:T(8,128)(2,1)S(1)} %all-to-all-done.2.r_ref, bf16[256,256]{1,0:T(8,128)(2,1)S(1)} %get-tuple-element.7.w1_ref, bf16[80,256]{1,0:T(8,128)(2,1)S(1)} %get-tuple-element.8.w2_ref), custom_call_target="tpu_custom_call" | custom-call | flops 268435456 | bytes 1048576 | tf_op jit(solution)/shard_map/pallas_call | solution.py:182
  (1 shorter events, 0.0 us)
Async XLA Ops:
  0.0 0.7 %copy-start.4 = (bf16[2,2,1024]{2,1,0:T(2,128)(2,1)S(1)}, bf16[2,2,1024]{2,1,0:T(2,128)(2,1)}, u32[]{:S(2)}) copy-start(bf16[2,2,1024]{2,1,0:T(2,128)(2,1)} %b_ref.1) | copy-start | bytes 24580
  1.5 6.8 %copy-start.3 = (bf16[1,8,1024]{2,1,0:T(8,128)(2,1)S(1)}, bf16[1,8,1024]{2,1,0:T(8,128)(2,1)}, u32[]{:S(2)}) copy-start(bf16[1,8,1024]{2,1,0:T(8,128)(2,1)} %param.8) | copy-start | bytes 49156
  1.5 12.9 %all-to-all-start = ((bf16[16,2,2,1024]{3,2,1,0:T(2,128)(2,1)}), bf16[16,2,2,1024]{3,2,1,0:T(2,128)(2,1)S(1)}, u32[]{:S(2)}, u32[]{:S(2)}) async-start(bf16[16,2,2,1024]{3,2,1,0:T(2,128)(2,1)} %shard_map.82), calls=%async_computation | async-start | bytes 262144 | tf_op jit(solution)/shard_map/all_to_all | solution.py:203
  8.4 4.3 %collective-permute-start.2 = (bf16[1,8,1024]{2,1,0:T(8,128)(2,1)S(1)}, bf16[1,8,1024]{2,1,0:T(8,128)(2,1)S(1)}, u32[]{:S(2)}, u32[]{:S(2)}) collective-permute-start(bf16[1,8,1024]{2,1,0:T(8,128)(2,1)S(1)} %copy-done.3), channel_id=1, source_target_pairs={{0,1},{1,0},{2,3},{3,2},{4,5},{5,4},{6,7},{7,6},{8,9},{9,8},{10,11... | collective-permute-start | bytes 49160 | tf_op jit(solution)/shard_map/ppermute | solution.py:205
  14.4 19.6 %all-to-all-start.1 = ((bf16[8,2,8,1024]{3,2,1,0:T(8,128)(2,1)}), bf16[8,2,8,1024]{3,2,1,0:T(8,128)(2,1)S(1)}, u32[]{:S(2)}, u32[]{:S(2)}) async-start(bf16[8,2,8,1024]{3,2,1,0:T(8,128)(2,1)} %shard_map.83), calls=%async_computation.1 | async-start | bytes 524288 | tf_op jit(solution)/shard_map/all_to_all | solution.py:217
  22.6 6.2 %collective-permute-start = (bf16[64,1024]{1,0:T(8,128)(2,1)S(1)}, bf16[64,1024]{1,0:T(8,128)(2,1)S(1)}, u32[]{:S(2)}, u32[]{:S(2)}) collective-permute-start(bf16[64,1024]{1,0:T(8,128)(2,1)S(1)} %reshape.15.own_ref), channel_id=1, source_target_pairs={{1,2},{3,4},{5,6},{7,8},{9,10},{11,12},{13,14},{2,1},{4,3},{6,5},{... | collective-permute-start | bytes 393224 | tf_op jit(solution)/shard_map/ppermute | solution.py:223
  23.3 10.7 %collective-permute-start.1 = (bf16[64,1024]{1,0:T(8,128)(2,1)S(1)}, bf16[64,1024]{1,0:T(8,128)(2,1)S(1)}, u32[]{:S(2)}, u32[]{:S(2)}) collective-permute-start(bf16[64,1024]{1,0:T(8,128)(2,1)S(1)} %reshape.15.own_ref), channel_id=1, source_target_pairs={{0,1},{1,0},{2,3},{3,2},{4,5},{5,4},{6,7},{7,6},{8,9},{9,8},{10,11... | collective-permute-start | bytes 393224 | tf_op jit(solution)/shard_map/ppermute | solution.py:222
  34.0 7.3 %copy-start.7 = (f32[8]{0:T(128)S(1)}, f32[8]{0:T(128)}, u32[]{:S(2)}) copy-start(f32[8]{0:T(128)} %param.11) | copy-start | bytes 100
  34.0 7.6 %copy-start.1 = (bf16[81,2048]{1,0:T(8,128)(2,1)S(1)}, bf16[81,2048]{1,0:T(8,128)(2,1)}, u32[]{:S(2)}) copy-start(bf16[81,2048]{1,0:T(8,128)(2,1)} %constant.27.clone.sel2_ref) | copy-start | bytes 995332
  34.0 7.6 %copy-start.2 = (bf16[81,81]{1,0:T(8,128)(2,1)S(1)}, bf16[81,81]{1,0:T(8,128)(2,1)}, u32[]{:S(2)}) copy-start(bf16[81,81]{1,0:T(8,128)(2,1)} %constant.25.clone.mirror_ref) | copy-start | bytes 39370
  35.0 6.6 %copy-start = (bf16[81,2048]{1,0:T(8,128)(2,1)S(1)}, bf16[81,2048]{1,0:T(8,128)(2,1)}, u32[]{:S(2)}) copy-start(bf16[81,2048]{1,0:T(8,128)(2,1)} %constant.26.clone.sel1_ref) | copy-start | bytes 995332
  35.0 12.7 %all-to-all-start.2 = ((bf16[16,36,128]{2,1,0:T(8,128)(2,1)}), bf16[16,36,128]{2,1,0:T(8,128)(2,1)S(1)}, u32[]{:S(2)}, u32[]{:S(2)}) async-start(bf16[16,36,128]{2,1,0:T(8,128)(2,1)} %shard_map.84), calls=%async_computation.2 | async-start | bytes 327680 | tf_op jit(solution)/shard_map/all_to_all | solution.py:258
  41.5 0.7 %copy-start.5 = (f32[8,81]{1,0:T(8,128)S(1)}, f32[8,81]{1,0:T(8,128)}, u32[]{:S(2)}) copy-start(f32[8,81]{1,0:T(8,128)} %cin_ref.1) | copy-start | bytes 7780
  41.5 0.7 %copy-start.6 = (f32[8,81]{1,0:T(8,128)S(1)}, f32[8,81]{1,0:T(8,128)}, u32[]{:S(2)}) copy-start(f32[8,81]{1,0:T(8,128)} %cout_ref.1) | copy-start | bytes 7780

commit v5 on v4

--- a/solution.py
+++ b/solution.py
@@ -100,14 +100,14 @@
     store_copies(v_ref, o_ref, out_sem)
 
 
-def volume_kernel(far_ref, own_ref, near_ref, a_ref, y_ref, o_ref, scr_ref, tmp_ref):
-    tall = jnp.concatenate([far_ref[...], own_ref[...], near_ref[...]], axis=0)
+def volume_kernel(halo_ref, own_ref, swap_ref, a_ref, slot_ref, o_ref, scr_ref, tmp_ref):
+    tall = jnp.concatenate([halo_ref[...], own_ref[...], swap_ref[...]], axis=0)
     scores = lax.dot_general(
         tall, a_ref[...], (((1,), (1,)), ((), ())), preferred_element_type=jnp.float32
     ) * (1024 ** -0.5)
     zeros = jnp.zeros((8, 128), jnp.float32)
-    far = 2 * y_ref[0]
-    for n, slot in enumerate((far, 1, 2 - far)):
+    first = 2 * slot_ref[0]
+    for n, slot in enumerate((first, 1, 2 - first)):
         scr_ref[slot, 0:8, :] = zeros
         scr_ref[slot, 8:72, :] = scores[64 * n : 64 * n + 64]
         scr_ref[slot, 72:80, :] = zeros
@@ -216,11 +216,16 @@
     )(feature_a[0], other[0], y_half)
     wide = lax.all_to_all(wide, "z", 0, 0, tiled=True)
     wide = wide.reshape(128, 1024)
-    near = [(2 * z + y, 2 * z + 1 - y) for z in range(8) for y in range(2)]
-    far = [(2 * z + 1, 2 * z + 2) for z in range(7)]
-    far += [(target, source) for source, target in far]
-    near = lax.ppermute(b, ("z", "yh"), near)
-    far = lax.ppermute(b, ("z", "yh"), far)
+    place = ("src", "z", "yh")
+    pairs = []
+    for index in range(0, 256, 16):
+        if index // 16 % 2:
+            pairs += [(index + t, index + (t ^ 1)) for t in range(16)]
+        else:
+            pairs += [(index + t, index + ((t - 1) ^ 1) + 1) for t in range(1, 15)]
+    halo = lax.ppermute(b, place, pairs)
+    swapped = lax.ppermute(halo, place, [(n, n ^ 16) for n in range(256)])
+    slot = (lax.axis_index("src") % 2) ^ lax.axis_index("yh")
     at = jnp.stack([lax.axis_index(("z", "yh")) * 2 - 1, lax.axis_index("src") * 2 - 1])
     w1, w2 = pl.pallas_call(
         weights_kernel,
@@ -254,7 +259,7 @@
         ],
         compiler_params=pltpu.CompilerParams(vmem_limit_bytes=16 << 20),
         cost_estimate=pl.CostEstimate(flops=1 << 26, bytes_accessed=1 << 20, transcendentals=0),
-    )(far, b, near, wide, y_half)
+    )(halo, b, swapped, wide, slot.reshape(1))
     pieces = lax.all_to_all(pieces, "src", 0, 0, tiled=True)
     out = call(
         consensus_kernel,

time: 50.5 us -> 50.4 us (level)
  starting transfers between devices: 30.2 us -> 29.3 us
  waiting for transfers between devices: 12.2 us -> 13 us
    all_to_all x1, waiting for transfers between devices: 0.01 us -> 1.79 us  [per_device(): wide = lax.all_to_all(wide, 'z', 0, 0, tiled=True)]
    ppermute x2, starting transfers between devices: 6.14 us -> 4.53 us  [the longest x1 4.53 us: per_device(): halo = lax.ppermute(b, place, pairs)]
    ppermute x2, waiting for transfers between devices: 5.23 us -> 4.32 us  [the longest x1 2.97 us: per_device(): halo = lax.ppermute(b, place, pairs)]
    all_to_all x1, starting transfers between devices: 6.35 us -> 7.09 us  [per_device(): pieces = lax.all_to_all(pieces, 'src', 0, 0, tiled=True)]
  transfers between devices with their start and end apart: 6 -> 6, of which waited for: 4 -> 6; matrix products, arithmetic and copies ran while one was open for 1% -> 1% of each run, Pallas kernels for 4% -> 4%
where the time goes in v5:
time: 50.4 us; the launch traced here: 49.9 us
  starting transfers between devices  29.3 us (58%)
  waiting for transfers between devices  13 us (26%)
  Pallas kernels  5.83 us (12%)
  local copies, waits for them, and re-layouts  1.54 us (3%)
    all_to_all x1, starting transfers between devices, per_device(): wide = lax.all_to_all(wide, 'z', 0, 0, tiled=True)  8.19 us
    all_to_all x1, starting transfers between devices, per_device(): pieces = lax.all_to_all(pieces, 'src', 0, 0, tiled=True)  7.09 us
    all_to_all x1, starting transfers between devices, per_device(): b = lax.all_to_all(b, 'src', 0, 0, tiled=True)  6.83 us
    ppermute x1, starting transfers between devices, per_device(): halo = lax.ppermute(b, place, pairs)  4.53 us
    all_to_all x1, waiting for transfers between devices, per_device(): pieces = lax.all_to_all(pieces, 'src', 0, 0, tiled=True)  4.37 us
    ppermute x1, waiting for transfers between devices, per_device(): halo = lax.ppermute(b, place, pairs)  2.97 us
    ppermute x1, starting transfers between devices, per_device(): other = lax.ppermute(feature_a, 'yh', [(0, 1), (1, 0)])  2.71 us
    pallas_call x1, Pallas kernels, call(): pl.pallas_call(kernel, out_shape=outs, in_specs=[VMEM] * len(args), out_s...  2.19 us
  transfers between devices with their start and end apart: 6, of which 6 were waited for; matrix products, arithmetic and copies ran while one was open for 1% of the time, Pallas kernels for 4%

profile of v5, /device:TPU:1, one launch (start us, length us, event | category | flops | bytes accessed | tf_op | source)
XLA Modules:
  0.0 49.9 jit_solution(5880704109315768813)
XLA Ops:
  0.0 0.0 copy-start.4
  0.0 0.7 %copy-done.4 = bf16[2,2,1024]{2,1,0:T(2,128)(2,1)S(1)} copy-done((bf16[2,2,1024]{2,1,0:T(2,128)(2,1)S(1)}, bf16[2,2,1024]{2,1,0:T(2,128)(2,1)}, u32[]{:S(2)}) %copy-start.4) | copy-done | bytes 8216
  0.7 0.8 %shard_map.82 = bf16[16,2,2,1024]{3,2,1,0:T(2,128)(2,1)} custom-call(bf16[2,2,1024]{2,1,0:T(2,128)(2,1)S(1)} %copy-done.4), custom_call_target="tpu_custom_call" | custom-call | tf_op jit(solution)/shard_map/pallas_call | solution.py:195
  1.5 0.0 copy-start.3
  1.5 6.8 %all-to-all-start = ((bf16[16,2,2,1024]{3,2,1,0:T(2,128)(2,1)}), bf16[16,2,2,1024]{3,2,1,0:T(2,128)(2,1)S(1)}, u32[]{:S(2)}, u32[]{:S(2)}) async-start(bf16[16,2,2,1024]{3,2,1,0:T(2,128)(2,1)} %shard_map.82), calls=%async_computation | async-start | bytes 262144 | tf_op jit(solution)/shard_map/all_to_all | solution.py:203
  8.3 0.0 copy-done.3
  8.4 2.7 %collective-permute-start.2 = (bf16[1,8,1024]{2,1,0:T(8,128)(2,1)S(1)}, bf16[1,8,1024]{2,1,0:T(8,128)(2,1)S(1)}, u32[]{:S(2)}, u32[]{:S(2)}) collective-permute-start(bf16[1,8,1024]{2,1,0:T(8,128)(2,1)S(1)} %copy-done.3), channel_id=1, source_target_pairs={{0,1},{1,0},{2,3},{3,2},{4,5},{5,4},{6,7},{7,6},{8,9},{9,8},{10,11... | collective-permute-start | bytes 49160 | tf_op jit(solution)/shard_map/ppermute | solution.py:205
  11.1 1.6 %collective-permute-done.2 = bf16[1,8,1024]{2,1,0:T(8,128)(2,1)S(1)} collective-permute-done((bf16[1,8,1024]{2,1,0:T(8,128)(2,1)S(1)}, bf16[1,8,1024]{2,1,0:T(8,128)(2,1)S(1)}, u32[]{:S(2)}, u32[]{:S(2)}) %collective-permute-start.2) | collective-permute-done | bytes 16416 | tf_op jit(solution)/shard_map/ppermute | solution.py:205
  12.7 0.8 %shard_map.83 = bf16[8,2,8,1024]{3,2,1,0:T(8,128)(2,1)} custom-call(bf16[8,1024]{1,0:T(8,128)(2,1)S(1)} %bitcast.9, bf16[8,1024]{1,0:T(8,128)(2,1)S(1)} %bitcast.10, s32[1]{0:T(128)} %bitcast.2.y_ref), custom_call_target="tpu_custom_call" | custom-call | tf_op jit(solution)/shard_map/pallas_call | solution.py:206
  13.4 1.0 %all-to-all-done = bf16[16,2,2,1024]{3,2,1,0:T(2,128)(2,1)S(1)} async-done(((bf16[16,2,2,1024]{3,2,1,0:T(2,128)(2,1)}), bf16[16,2,2,1024]{3,2,1,0:T(2,128)(2,1)S(1)}, u32[]{:S(2)}, u32[]{:S(2)}) %all-to-all-start) | async-done | bytes 131104 | tf_op jit(solution)/shard_map/all_to_all | solution.py:203
  14.4 8.2 %all-to-all-start.1 = ((bf16[8,2,8,1024]{3,2,1,0:T(8,128)(2,1)}), bf16[8,2,8,1024]{3,2,1,0:T(8,128)(2,1)S(1)}, u32[]{:S(2)}, u32[]{:S(2)}) async-start(bf16[8,2,8,1024]{3,2,1,0:T(8,128)(2,1)} %shard_map.83), calls=%async_computation.1 | async-start | bytes 524288 | tf_op jit(solution)/shard_map/all_to_all | solution.py:217
  22.6 0.1 reshape.18.own_ref
  22.6 4.5 %collective-permute-start = (bf16[64,1024]{1,0:T(8,128)(2,1)S(1)}, bf16[64,1024]{1,0:T(8,128)(2,1)S(1)}, u32[]{:S(2)}, u32[]{:S(2)}) collective-permute-start(bf16[64,1024]{1,0:T(8,128)(2,1)S(1)} %reshape.18.own_ref), channel_id=1, source_target_pairs={{1,2},{2,1},{3,4},{4,3},{5,6},{6,5},{7,8},{8,7},{9,10},{10,9},{11,... | collective-permute-start | bytes 393224 | tf_op jit(solution)/shard_map/ppermute | solution.py:226
  27.2 3.0 %collective-permute-done.halo_ref = bf16[64,1024]{1,0:T(8,128)(2,1)S(1)} collective-permute-done((bf16[64,1024]{1,0:T(8,128)(2,1)S(1)}, bf16[64,1024]{1,0:T(8,128)(2,1)S(1)}, u32[]{:S(2)}, u32[]{:S(2)}) %collective-permute-start) | collective-permute-done | bytes 131104 | tf_op jit(solution)/shard_map/ppermute | solution.py:226
  30.2 0.0 collective-permute-start.1
  30.2 1.3 %collective-permute-done.1.swap_ref = bf16[64,1024]{1,0:T(8,128)(2,1)S(1)} collective-permute-done((bf16[64,1024]{1,0:T(8,128)(2,1)S(1)}, bf16[64,1024]{1,0:T(8,128)(2,1)S(1)}, u32[]{:S(2)}, u32[]{:S(2)}) %collective-permute-start.1) | collective-permute-done | bytes 131104 | tf_op jit(solution)/shard_map/ppermute | solution.py:227
  31.5 1.8 %all-to-all-done.1 = bf16[8,2,8,1024]{3,2,1,0:T(8,128)(2,1)S(1)} async-done(((bf16[8,2,8,1024]{3,2,1,0:T(8,128)(2,1)}), bf16[8,2,8,1024]{3,2,1,0:T(8,128)(2,1)S(1)}, u32[]{:S(2)}, u32[]{:S(2)}) %all-to-all-start.1) | async-done | bytes 262176 | tf_op jit(solution)/shard_map/all_to_all | solution.py:217
  33.3 0.0 copy-start.7
  33.3 0.0 copy-start.1
  33.3 0.0 copy-start.2
  33.3 1.0 %shard_map.84 = bf16[16,36,128]{2,1,0:T(8,128)(2,1)} custom-call(bf16[64,1024]{1,0:T(8,128)(2,1)S(1)} %collective-permute-done.halo_ref, bf16[64,1024]{1,0:T(8,128)(2,1)S(1)} %reshape.18.own_ref, bf16[64,1024]{1,0:T(8,128)(2,1)S(1)} %collective-permute-done.1.swap_ref, bf16[128,1024]{1,0:T(8,128)(2,1)S(1)} %bitcast.8, s32[1]{0:T(128)} %bitcast.4.slot_ref), custom_call_target="tpu_custom_call" | custom-call | flops 67108864 | bytes 1048576 | tf_op jit(solution)/shard_map/pallas_call | solution.py:251
  34.3 0.0 copy-start
  34.3 7.1 %all-to-all-start.2 = ((bf16[16,36,128]{2,1,0:T(8,128)(2,1)}), bf16[16,36,128]{2,1,0:T(8,128)(2,1)S(1)}, u32[]{:S(2)}, u32[]{:S(2)}) async-start(bf16[16,36,128]{2,1,0:T(8,128)(2,1)} %shard_map.84), calls=%async_computation.2 | async-start | bytes 327680 | tf_op jit(solution)/shard_map/all_to_all | solution.py:263
  41.4 0.0 copy-done.7
  41.4 0.1 broadcast_in_dim.11
  41.5 0.1 pad_add_fusion.at_ref
  41.5 0.0 copy-start.5
  41.5 0.0 copy-start.6
  41.5 0.1 broadcast_in_dim.12.bias_ref
  41.6 0.0 copy-done.1
  41.6 0.0 copy-done.2
  41.6 0.0 copy-done
  41.6 0.6 %copy-done.5 = f32[8,81]{1,0:T(8,128)S(1)} copy-done((f32[8,81]{1,0:T(8,128)S(1)}, f32[8,81]{1,0:T(8,128)}, u32[]{:S(2)}) %copy-start.5) | copy-done | bytes 2616
  42.2 0.0 copy-done.6
  42.2 1.1 %shard_map.85 = (bf16[256,256]{1,0:T(8,128)(2,1)S(1)}, bf16[80,256]{1,0:T(8,128)(2,1)S(1)}) custom-call(f32[8,81]{1,0:T(8,128)S(1)} %copy-done.5, f32[8,81]{1,0:T(8,128)S(1)} %copy-done.6, bf16[81,81]{1,0:T(8,128)(2,1)S(1)} %copy-done.2, bf16[81,2048]{1,0:T(8,128)(2,1)S(1)} %copy-done, bf16[81,2048]{1,0:T(8,128)(2,1)S(1)} %copy-done.1, ...), custom_call_target="tpu_custom_call" | custom-call | flops 16777216 | bytes 1048576 | tf_op jit(solution)/shard_map/pallas_call | solution.py:230
  43.3 4.4 %all-to-all-done.2.r_ref = bf16[16,36,128]{2,1,0:T(8,128)(2,1)S(1)} async-done(((bf16[16,36,128]{2,1,0:T(8,128)(2,1)}), bf16[16,36,128]{2,1,0:T(8,128)(2,1)S(1)}, u32[]{:S(2)}, u32[]{:S(2)}) %all-to-all-start.2) | async-done | bytes 147488 | tf_op jit(solution)/shard_map/all_to_all | solution.py:263
  47.7 2.2 %shard_map.86 = f32[64,128]{1,0:T(8,128)} custom-call(bf16[16,36,128]{2,1,0:T(8,128)(2,1)S(1)} %all-to-all-done.2.r_ref, bf16[256,256]{1,0:T(8,128)(2,1)S(1)} %get-tuple-element.7.w1_ref, bf16[80,256]{1,0:T(8,128)(2,1)S(1)} %get-tuple-element.8.w2_ref), custom_call_target="tpu_custom_call" | custom-call | flops 268435456 | bytes 1048576 | tf_op jit(solution)/shard_map/pallas_call | solution.py:182
  (1 shorter events, 0.0 us)
Async XLA Ops:
  0.0 0.7 %copy-start.4 = (bf16[2,2,1024]{2,1,0:T(2,128)(2,1)S(1)}, bf16[2,2,1024]{2,1,0:T(2,128)(2,1)}, u32[]{:S(2)}) copy-start(bf16[2,2,1024]{2,1,0:T(2,128)(2,1)} %b_ref.1) | copy-start | bytes 24580
  1.5 6.8 %copy-start.3 = (bf16[1,8,1024]{2,1,0:T(8,128)(2,1)S(1)}, bf16[1,8,1024]{2,1,0:T(8,128)(2,1)}, u32[]{:S(2)}) copy-start(bf16[1,8,1024]{2,1,0:T(8,128)(2,1)} %param.8) | copy-start | bytes 49156
  1.5 12.9 %all-to-all-start = ((bf16[16,2,2,1024]{3,2,1,0:T(2,128)(2,1)}), bf16[16,2,2,1024]{3,2,1,0:T(2,128)(2,1)S(1)}, u32[]{:S(2)}, u32[]{:S(2)}) async-start(bf16[16,2,2,1024]{3,2,1,0:T(2,128)(2,1)} %shard_map.82), calls=%async_computation | async-start | bytes 262144 | tf_op jit(solution)/shard_map/all_to_all | solution.py:203
  8.4 4.3 %collective-permute-start.2 = (bf16[1,8,1024]{2,1,0:T(8,128)(2,1)S(1)}, bf16[1,8,1024]{2,1,0:T(8,128)(2,1)S(1)}, u32[]{:S(2)}, u32[]{:S(2)}) collective-permute-start(bf16[1,8,1024]{2,1,0:T(8,128)(2,1)S(1)} %copy-done.3), channel_id=1, source_target_pairs={{0,1},{1,0},{2,3},{3,2},{4,5},{5,4},{6,7},{7,6},{8,9},{9,8},{10,11... | collective-permute-start | bytes 49160 | tf_op jit(solution)/shard_map/ppermute | solution.py:205
  14.4 18.9 %all-to-all-start.1 = ((bf16[8,2,8,1024]{3,2,1,0:T(8,128)(2,1)}), bf16[8,2,8,1024]{3,2,1,0:T(8,128)(2,1)S(1)}, u32[]{:S(2)}, u32[]{:S(2)}) async-start(bf16[8,2,8,1024]{3,2,1,0:T(8,128)(2,1)} %shard_map.83), calls=%async_computation.1 | async-start | bytes 524288 | tf_op jit(solution)/shard_map/all_to_all | solution.py:217
  22.6 7.5 %collective-permute-start = (bf16[64,1024]{1,0:T(8,128)(2,1)S(1)}, bf16[64,1024]{1,0:T(8,128)(2,1)S(1)}, u32[]{:S(2)}, u32[]{:S(2)}) collective-permute-start(bf16[64,1024]{1,0:T(8,128)(2,1)S(1)} %reshape.18.own_ref), channel_id=1, source_target_pairs={{1,2},{2,1},{3,4},{4,3},{5,6},{6,5},{7,8},{8,7},{9,10},{10,9},{11,... | collective-permute-start | bytes 393224 | tf_op jit(solution)/shard_map/ppermute | solution.py:226
  30.2 1.3 %collective-permute-start.1 = (bf16[64,1024]{1,0:T(8,128)(2,1)S(1)}, bf16[64,1024]{1,0:T(8,128)(2,1)S(1)}, u32[]{:S(2)}, u32[]{:S(2)}) collective-permute-start(bf16[64,1024]{1,0:T(8,128)(2,1)S(1)} %collective-permute-done.halo_ref), channel_id=1, source_target_pairs={{0,16},{1,17},{2,18},{3,19},{4,20},{5,21},{6,22},{7,23},{8,24},{9,... | collective-permute-start | bytes 393224 | tf_op jit(solution)/shard_map/ppermute | solution.py:227
  33.3 8.1 %copy-start.7 = (f32[8]{0:T(128)S(1)}, f32[8]{0:T(128)}, u32[]{:S(2)}) copy-start(f32[8]{0:T(128)} %param.11) | copy-start | bytes 100
  33.3 8.3 %copy-start.1 = (bf16[81,2048]{1,0:T(8,128)(2,1)S(1)}, bf16[81,2048]{1,0:T(8,128)(2,1)}, u32[]{:S(2)}) copy-start(bf16[81,2048]{1,0:T(8,128)(2,1)} %constant.38.clone.sel2_ref) | copy-start | bytes 995332
  33.3 8.3 %copy-start.2 = (bf16[81,81]{1,0:T(8,128)(2,1)S(1)}, bf16[81,81]{1,0:T(8,128)(2,1)}, u32[]{:S(2)}) copy-start(bf16[81,81]{1,0:T(8,128)(2,1)} %constant.36.clone.mirror_ref) | copy-start | bytes 39370
  34.3 7.3 %copy-start = (bf16[81,2048]{1,0:T(8,128)(2,1)S(1)}, bf16[81,2048]{1,0:T(8,128)(2,1)}, u32[]{:S(2)}) copy-start(bf16[81,2048]{1,0:T(8,128)(2,1)} %constant.37.clone.sel1_ref) | copy-start | bytes 995332
  34.3 13.4 %all-to-all-start.2 = ((bf16[16,36,128]{2,1,0:T(8,128)(2,1)}), bf16[16,36,128]{2,1,0:T(8,128)(2,1)S(1)}, u32[]{:S(2)}, u32[]{:S(2)}) async-start(bf16[16,36,128]{2,1,0:T(8,128)(2,1)} %shard_map.84), calls=%async_computation.2 | async-start | bytes 327680 | tf_op jit(solution)/shard_map/all_to_all | solution.py:263
  41.5 0.7 %copy-start.5 = (f32[8,81]{1,0:T(8,128)S(1)}, f32[8,81]{1,0:T(8,128)}, u32[]{:S(2)}) copy-start(f32[8,81]{1,0:T(8,128)} %cin_ref.1) | copy-start | bytes 7780
  41.5 0.7 %copy-start.6 = (f32[8,81]{1,0:T(8,128)S(1)}, f32[8,81]{1,0:T(8,128)}, u32[]{:S(2)}) copy-start(f32[8,81]{1,0:T(8,128)} %cout_ref.1) | copy-start | bytes 7780

commit v6 on v5

--- a/solution.py
+++ b/solution.py
@@ -78,26 +78,18 @@
     w2_ref[...] = jnp.concatenate(rows, axis=0).astype(jnp.bfloat16)
 
 
-def store_copies(source, target, sems):
-    stores = [
-        pltpu.make_async_copy(source, target.at[n], sems.at[n]) for n in range(target.shape[0])
-    ]
-    for store in stores:
-        store.start()
-    for store in stores:
-        store.wait()
-
-
-def b_copies_kernel(b_ref, o_ref, out_sem):
-    store_copies(b_ref, o_ref, out_sem)
-
-
-def a_copies_kernel(mine_ref, other_ref, y_ref, o_ref, v_ref, out_sem):
+def b_copies_kernel(b_ref, o_ref):
+    for n in range(o_ref.shape[0]):
+        o_ref[n] = b_ref[...]
+
+
+def a_copies_kernel(mine_ref, other_ref, y_ref, o_ref):
     first = y_ref[0] == 0
     mine, other = mine_ref[...], other_ref[...]
-    v_ref[0] = jnp.where(first, mine, other)
-    v_ref[1] = jnp.where(first, other, mine)
-    store_copies(v_ref, o_ref, out_sem)
+    low, high = jnp.where(first, mine, other), jnp.where(first, other, mine)
+    for n in range(o_ref.shape[0]):
+        o_ref[n, 0] = low
+        o_ref[n, 1] = high
 
 
 def volume_kernel(halo_ref, own_ref, swap_ref, a_ref, slot_ref, o_ref, scr_ref, tmp_ref):
@@ -117,12 +109,13 @@
         o_ref[s] = tmp_ref[s, 0:36, :].astype(jnp.bfloat16)
 
 
-def consensus_kernel(r_ref, w1_ref, w2_ref, o_ref, rf_ref, xs_ref, ps_ref):
+def consensus_kernel(r_ref, w1_ref, w2_ref, y_ref, o_ref, rf_ref, xs_ref, ps_ref):
     xs_ref[0:80, :] = jnp.zeros((80, 256), jnp.bfloat16)
     xs_ref[1360:1456, :] = jnp.zeros((96, 256), jnp.bfloat16)
     sublane = lax.broadcasted_iota(jnp.int32, (8, 128), 0)
+    mine = ((lax.broadcasted_iota(jnp.int32, (36, 128), 1) >> 3) & 1) == y_ref[0]
     for i in range(16):
-        rf_ref[i] = r_ref[i].astype(jnp.float32)
+        rf_ref[i] = jnp.where(mine, r_ref[i].astype(jnp.float32), r_ref[i ^ 8].astype(jnp.float32))
         for half in range(2):
             rows = [rf_ref[i, pl.ds(half * 12 + d, 8), :] for d in range(0, 24, 8)]
             rows = [shifted(x, s) for s in SHIFTS for x in rows]
@@ -175,19 +168,6 @@
 
 VMEM = pl.BlockSpec(memory_space=pltpu.VMEM)
 SMEM = pl.BlockSpec(memory_space=pltpu.SMEM)
-HBM = pl.BlockSpec(memory_space=pltpu.HBM)
-
-
-def call(kernel, outs, scratch, flops, *args):
-    return pl.pallas_call(
-        kernel,
-        out_shape=outs,
-        in_specs=[VMEM] * len(args),
-        out_specs=jax.tree.map(lambda _: VMEM, outs),
-        scratch_shapes=scratch,
-        compiler_params=pltpu.CompilerParams(vmem_limit_bytes=16 << 20),
-        cost_estimate=pl.CostEstimate(flops=flops, bytes_accessed=1 << 20, transcendentals=0),
-    )(*args)
 
 
 def per_device(feature_a, feature_b, conv_in, bias_in, conv_out):
@@ -196,22 +176,19 @@
         b_copies_kernel,
         out_shape=jax.ShapeDtypeStruct((16, 2, 2, 1024), jnp.bfloat16),
         in_specs=[VMEM],
-        out_specs=HBM,
-        scratch_shapes=[pltpu.SemaphoreType.DMA((16,))],
+        out_specs=VMEM,
         compiler_params=pltpu.CompilerParams(vmem_limit_bytes=16 << 20),
     )(feature_b)
     b = lax.all_to_all(b, "src", 0, 0, tiled=True)
     b = b.reshape(64, 1024)
-    other = lax.ppermute(feature_a, "yh", [(0, 1), (1, 0)])
+    other = lax.ppermute(
+        feature_a, ("src", "z", "yh"), [(n, n ^ 129) for n in range(256)]
+    )
     wide = pl.pallas_call(
         a_copies_kernel,
         out_shape=jax.ShapeDtypeStruct((8, 2, 8, 1024), jnp.bfloat16),
         in_specs=[VMEM, VMEM, SMEM],
-        out_specs=HBM,
-        scratch_shapes=[
-            pltpu.VMEM((2, 8, 1024), jnp.bfloat16),
-            pltpu.SemaphoreType.DMA((8,)),
-        ],
+        out_specs=VMEM,
         compiler_params=pltpu.CompilerParams(vmem_limit_bytes=16 << 20),
     )(feature_a[0], other[0], y_half)
     wide = lax.all_to_all(wide, "z", 0, 0, tiled=True)
@@ -261,19 +238,19 @@
         cost_estimate=pl.CostEstimate(flops=1 << 26, bytes_accessed=1 << 20, transcendentals=0),
     )(halo, b, swapped, wide, slot.reshape(1))
     pieces = lax.all_to_all(pieces, "src", 0, 0, tiled=True)
-    out = call(
+    out = pl.pallas_call(
         consensus_kernel,
-        jax.ShapeDtypeStruct((64, 128), jnp.float32),
-        [
+        out_shape=jax.ShapeDtypeStruct((64, 128), jnp.float32),
+        in_specs=[VMEM] * 3 + [SMEM],
+        out_specs=VMEM,
+        scratch_shapes=[
             pltpu.VMEM((16, 36, 128), jnp.float32),
             pltpu.VMEM((1456, 256), jnp.bfloat16),
             pltpu.VMEM((720, 128), jnp.float32),
         ],
-        1 << 28,
-        pieces,
-        w1,
-        w2,
-    )
+        compiler_params=pltpu.CompilerParams(vmem_limit_bytes=16 << 20),
+        cost_estimate=pl.CostEstimate(flops=1 << 28, bytes_accessed=1 << 20, transcendentals=0),
+    )(pieces, w1, w2, y_half)
     return out.reshape(2, 2, 16, 128)
 
 

time: 50.4 us -> 48.9 us (0.970)
  starting transfers between devices: 29.3 us -> 28.1 us
    all_to_all x1, starting transfers between devices: 7.09 us -> 5.56 us  [per_device(): pieces = lax.all_to_all(pieces, 'src', 0, 0, tiled=True)]
where the time goes in v6:
time: 48.9 us; the launch traced here: 48.4 us
  starting transfers between devices  28.1 us (57%)
  waiting for transfers between devices  13 us (27%)
  Pallas kernels  5.62 us (11%)
  local copies, waits for them, and re-layouts  1.54 us (3%)
    all_to_all x1, starting transfers between devices, per_device(): wide = lax.all_to_all(wide, 'z', 0, 0, tiled=True)  8.19 us
    all_to_all x1, starting transfers between devices, per_device(): b = lax.all_to_all(b, 'src', 0, 0, tiled=True)  6.95 us
    all_to_all x1, starting transfers between devices, per_device(): pieces = lax.all_to_all(pieces, 'src', 0, 0, tiled=True)  5.56 us
    ppermute x1, starting transfers between devices, per_device(): halo = lax.ppermute(b, place, pairs)  4.53 us
    all_to_all x1, waiting for transfers between devices, per_device(): pieces = lax.all_to_all(pieces, 'src', 0, 0, tiled=True)  4.45 us
    ppermute x1, waiting for transfers between devices, per_device(): halo = lax.ppermute(b, place, pairs)  2.97 us
    ppermute x1, starting transfers between devices, per_device(): lax.ppermute(feature_a, ('src', 'z', 'yh'), [(n, n ^ 129) for n in range(...  2.88 us
    pallas_call x1, Pallas kernels, per_device(): pl.pallas_call(consensus_kernel, out_shape=jax.ShapeDtypeStruct((64, 128)...  2.18 us
  transfers between devices with their start and end apart: 6, of which 6 were waited for; matrix products, arithmetic and copies ran while one was open for 1% of the time, Pallas kernels for 4%

profile of v6, /device:TPU:1, one launch (start us, length us, event | category | flops | bytes accessed | tf_op | source)
XLA Modules:
  0.0 48.4 jit_solution(9880853128584947653)
XLA Ops:
  0.0 0.0 copy-start.4
  0.0 0.7 %copy-done.4 = bf16[2,2,1024]{2,1,0:T(2,128)(2,1)S(1)} copy-done((bf16[2,2,1024]{2,1,0:T(2,128)(2,1)S(1)}, bf16[2,2,1024]{2,1,0:T(2,128)(2,1)}, u32[]{:S(2)}) %copy-start.4) | copy-done | bytes 8216
  0.7 0.7 %shard_map.82 = bf16[16,2,2,1024]{3,2,1,0:T(2,128)(2,1)} custom-call(bf16[2,2,1024]{2,1,0:T(2,128)(2,1)S(1)} %copy-done.4), custom_call_target="tpu_custom_call" | custom-call | tf_op jit(solution)/shard_map/pallas_call | solution.py:175
  1.4 0.0 copy-start.3
  1.4 6.9 %all-to-all-start = ((bf16[16,2,2,1024]{3,2,1,0:T(2,128)(2,1)}), bf16[16,2,2,1024]{3,2,1,0:T(2,128)(2,1)S(1)}, u32[]{:S(2)}, u32[]{:S(2)}) async-start(bf16[16,2,2,1024]{3,2,1,0:T(2,128)(2,1)} %shard_map.82), calls=%async_computation | async-start | bytes 262144 | tf_op jit(solution)/shard_map/all_to_all | solution.py:182
  8.3 0.0 copy-done.3
  8.3 2.9 %collective-permute-start.2 = (bf16[1,8,1024]{2,1,0:T(8,128)(2,1)S(1)}, bf16[1,8,1024]{2,1,0:T(8,128)(2,1)S(1)}, u32[]{:S(2)}, u32[]{:S(2)}) collective-permute-start(bf16[1,8,1024]{2,1,0:T(8,128)(2,1)S(1)} %copy-done.3), channel_id=1, source_target_pairs={{0,129},{1,128},{2,131},{3,130},{4,133},{5,132},{6,135},{7,134},{8... | collective-permute-start | bytes 49160 | tf_op jit(solution)/shard_map/ppermute | solution.py:184
  11.2 1.4 %collective-permute-done.2 = bf16[1,8,1024]{2,1,0:T(8,128)(2,1)S(1)} collective-permute-done((bf16[1,8,1024]{2,1,0:T(8,128)(2,1)S(1)}, bf16[1,8,1024]{2,1,0:T(8,128)(2,1)S(1)}, u32[]{:S(2)}, u32[]{:S(2)}) %collective-permute-start.2) | collective-permute-done | bytes 16416 | tf_op jit(solution)/shard_map/ppermute | solution.py:184
  12.6 0.7 %shard_map.83 = bf16[8,2,8,1024]{3,2,1,0:T(8,128)(2,1)} custom-call(bf16[8,1024]{1,0:T(8,128)(2,1)S(1)} %bitcast.9, bf16[8,1024]{1,0:T(8,128)(2,1)S(1)} %bitcast.10, s32[1]{0:T(128)} %bitcast.2.y_ref), custom_call_target="tpu_custom_call" | custom-call | tf_op jit(solution)/shard_map/pallas_call | solution.py:187
  13.3 1.1 %all-to-all-done = bf16[16,2,2,1024]{3,2,1,0:T(2,128)(2,1)S(1)} async-done(((bf16[16,2,2,1024]{3,2,1,0:T(2,128)(2,1)}), bf16[16,2,2,1024]{3,2,1,0:T(2,128)(2,1)S(1)}, u32[]{:S(2)}, u32[]{:S(2)}) %all-to-all-start) | async-done | bytes 131104 | tf_op jit(solution)/shard_map/all_to_all | solution.py:182
  14.4 8.2 %all-to-all-start.1 = ((bf16[8,2,8,1024]{3,2,1,0:T(8,128)(2,1)}), bf16[8,2,8,1024]{3,2,1,0:T(8,128)(2,1)S(1)}, u32[]{:S(2)}, u32[]{:S(2)}) async-start(bf16[8,2,8,1024]{3,2,1,0:T(8,128)(2,1)} %shard_map.83), calls=%async_computation.1 | async-start | bytes 524288 | tf_op jit(solution)/shard_map/all_to_all | solution.py:194
  22.5 0.1 reshape.18.own_ref
  22.6 4.5 %collective-permute-start = (bf16[64,1024]{1,0:T(8,128)(2,1)S(1)}, bf16[64,1024]{1,0:T(8,128)(2,1)S(1)}, u32[]{:S(2)}, u32[]{:S(2)}) collective-permute-start(bf16[64,1024]{1,0:T(8,128)(2,1)S(1)} %reshape.18.own_ref), channel_id=1, source_target_pairs={{1,2},{2,1},{3,4},{4,3},{5,6},{6,5},{7,8},{8,7},{9,10},{10,9},{11,... | collective-permute-start | bytes 393224 | tf_op jit(solution)/shard_map/ppermute | solution.py:203
  27.1 3.0 %collective-permute-done.halo_ref = bf16[64,1024]{1,0:T(8,128)(2,1)S(1)} collective-permute-done((bf16[64,1024]{1,0:T(8,128)(2,1)S(1)}, bf16[64,1024]{1,0:T(8,128)(2,1)S(1)}, u32[]{:S(2)}, u32[]{:S(2)}) %collective-permute-start) | collective-permute-done | bytes 131104 | tf_op jit(solution)/shard_map/ppermute | solution.py:203
  30.1 0.0 collective-permute-start.1
  30.1 1.3 %collective-permute-done.1.swap_ref = bf16[64,1024]{1,0:T(8,128)(2,1)S(1)} collective-permute-done((bf16[64,1024]{1,0:T(8,128)(2,1)S(1)}, bf16[64,1024]{1,0:T(8,128)(2,1)S(1)}, u32[]{:S(2)}, u32[]{:S(2)}) %collective-permute-start.1) | collective-permute-done | bytes 131104 | tf_op jit(solution)/shard_map/ppermute | solution.py:204
  31.5 1.8 %all-to-all-done.1 = bf16[8,2,8,1024]{3,2,1,0:T(8,128)(2,1)S(1)} async-done(((bf16[8,2,8,1024]{3,2,1,0:T(8,128)(2,1)}), bf16[8,2,8,1024]{3,2,1,0:T(8,128)(2,1)S(1)}, u32[]{:S(2)}, u32[]{:S(2)}) %all-to-all-start.1) | async-done | bytes 262176 | tf_op jit(solution)/shard_map/all_to_all | solution.py:194
  33.2 0.0 copy-start.7
  33.3 0.0 copy-start.1
  33.3 0.0 copy-start.2
  33.3 1.0 %shard_map.84 = bf16[16,36,128]{2,1,0:T(8,128)(2,1)} custom-call(bf16[64,1024]{1,0:T(8,128)(2,1)S(1)} %collective-permute-done.halo_ref, bf16[64,1024]{1,0:T(8,128)(2,1)S(1)} %reshape.18.own_ref, bf16[64,1024]{1,0:T(8,128)(2,1)S(1)} %collective-permute-done.1.swap_ref, bf16[128,1024]{1,0:T(8,128)(2,1)S(1)} %bitcast.8, s32[1]{0:T(128)} %bitcast.4.slot_ref), custom_call_target="tpu_custom_call" | custom-call | flops 67108864 | bytes 1048576 | tf_op jit(solution)/shard_map/pallas_call | solution.py:228
  34.2 0.0 copy-start
  34.2 5.6 %all-to-all-start.2 = ((bf16[16,36,128]{2,1,0:T(8,128)(2,1)}), bf16[16,36,128]{2,1,0:T(8,128)(2,1)S(1)}, u32[]{:S(2)}, u32[]{:S(2)}) async-start(bf16[16,36,128]{2,1,0:T(8,128)(2,1)} %shard_map.84), calls=%async_computation.2 | async-start | bytes 327680 | tf_op jit(solution)/shard_map/all_to_all | solution.py:240
  39.8 0.0 copy-done.7
  39.8 0.1 broadcast_in_dim.11
  39.9 0.1 pad_add_fusion.at_ref
  40.0 0.0 copy-start.5
  40.0 0.0 copy-start.6
  40.0 0.1 broadcast_in_dim.12.bias_ref
  40.1 0.0 copy-done.1
  40.1 0.0 copy-done.2
  40.1 0.0 copy-done
  40.1 0.6 %copy-done.5 = f32[8,81]{1,0:T(8,128)S(1)} copy-done((f32[8,81]{1,0:T(8,128)S(1)}, f32[8,81]{1,0:T(8,128)}, u32[]{:S(2)}) %copy-start.5) | copy-done | bytes 2616
  40.7 0.0 copy-done.6
  40.7 1.1 %shard_map.85 = (bf16[256,256]{1,0:T(8,128)(2,1)S(1)}, bf16[80,256]{1,0:T(8,128)(2,1)S(1)}) custom-call(f32[8,81]{1,0:T(8,128)S(1)} %copy-done.5, f32[8,81]{1,0:T(8,128)S(1)} %copy-done.6, bf16[81,81]{1,0:T(8,128)(2,1)S(1)} %copy-done.2, bf16[81,2048]{1,0:T(8,128)(2,1)S(1)} %copy-done, bf16[81,2048]{1,0:T(8,128)(2,1)S(1)} %copy-done.1, ...), custom_call_target="tpu_custom_call" | custom-call | flops 16777216 | bytes 1048576 | tf_op jit(solution)/shard_map/pallas_call | solution.py:207
  41.8 4.4 %all-to-all-done.2.r_ref = bf16[16,36,128]{2,1,0:T(8,128)(2,1)S(1)} async-done(((bf16[16,36,128]{2,1,0:T(8,128)(2,1)}), bf16[16,36,128]{2,1,0:T(8,128)(2,1)S(1)}, u32[]{:S(2)}, u32[]{:S(2)}) %all-to-all-start.2) | async-done | bytes 147488 | tf_op jit(solution)/shard_map/all_to_all | solution.py:240
  46.2 2.2 %shard_map.86 = f32[64,128]{1,0:T(8,128)} custom-call(bf16[16,36,128]{2,1,0:T(8,128)(2,1)S(1)} %all-to-all-done.2.r_ref, bf16[256,256]{1,0:T(8,128)(2,1)S(1)} %get-tuple-element.7.w1_ref, bf16[80,256]{1,0:T(8,128)(2,1)S(1)} %get-tuple-element.8.w2_ref, s32[1]{0:T(128)} %bitcast.2.y_ref), custom_call_target="tpu_custom_call" | custom-call | flops 268435456 | bytes 1048576 | tf_op jit(solution)/shard_map/pallas_call | solution.py:241
  (1 shorter events, 0.0 us)
Async XLA Ops:
  0.0 0.7 %copy-start.4 = (bf16[2,2,1024]{2,1,0:T(2,128)(2,1)S(1)}, bf16[2,2,1024]{2,1,0:T(2,128)(2,1)}, u32[]{:S(2)}) copy-start(bf16[2,2,1024]{2,1,0:T(2,128)(2,1)} %b_ref.1) | copy-start | bytes 24580
  1.4 7.0 %copy-start.3 = (bf16[1,8,1024]{2,1,0:T(8,128)(2,1)S(1)}, bf16[1,8,1024]{2,1,0:T(8,128)(2,1)}, u32[]{:S(2)}) copy-start(bf16[1,8,1024]{2,1,0:T(8,128)(2,1)} %param.8) | copy-start | bytes 49156
  1.4 13.0 %all-to-all-start = ((bf16[16,2,2,1024]{3,2,1,0:T(2,128)(2,1)}), bf16[16,2,2,1024]{3,2,1,0:T(2,128)(2,1)S(1)}, u32[]{:S(2)}, u32[]{:S(2)}) async-start(bf16[16,2,2,1024]{3,2,1,0:T(2,128)(2,1)} %shard_map.82), calls=%async_computation | async-start | bytes 262144 | tf_op jit(solution)/shard_map/all_to_all | solution.py:182
  8.3 4.3 %collective-permute-start.2 = (bf16[1,8,1024]{2,1,0:T(8,128)(2,1)S(1)}, bf16[1,8,1024]{2,1,0:T(8,128)(2,1)S(1)}, u32[]{:S(2)}, u32[]{:S(2)}) collective-permute-start(bf16[1,8,1024]{2,1,0:T(8,128)(2,1)S(1)} %copy-done.3), channel_id=1, source_target_pairs={{0,129},{1,128},{2,131},{3,130},{4,133},{5,132},{6,135},{7,134},{8... | collective-permute-start | bytes 49160 | tf_op jit(solution)/shard_map/ppermute | solution.py:184
  14.4 18.9 %all-to-all-start.1 = ((bf16[8,2,8,1024]{3,2,1,0:T(8,128)(2,1)}), bf16[8,2,8,1024]{3,2,1,0:T(8,128)(2,1)S(1)}, u32[]{:S(2)}, u32[]{:S(2)}) async-start(bf16[8,2,8,1024]{3,2,1,0:T(8,128)(2,1)} %shard_map.83), calls=%async_computation.1 | async-start | bytes 524288 | tf_op jit(solution)/shard_map/all_to_all | solution.py:194
  22.6 7.5 %collective-permute-start = (bf16[64,1024]{1,0:T(8,128)(2,1)S(1)}, bf16[64,1024]{1,0:T(8,128)(2,1)S(1)}, u32[]{:S(2)}, u32[]{:S(2)}) collective-permute-start(bf16[64,1024]{1,0:T(8,128)(2,1)S(1)} %reshape.18.own_ref), channel_id=1, source_target_pairs={{1,2},{2,1},{3,4},{4,3},{5,6},{6,5},{7,8},{8,7},{9,10},{10,9},{11,... | collective-permute-start | bytes 393224 | tf_op jit(solution)/shard_map/ppermute | solution.py:203
  30.1 1.3 %collective-permute-start.1 = (bf16[64,1024]{1,0:T(8,128)(2,1)S(1)}, bf16[64,1024]{1,0:T(8,128)(2,1)S(1)}, u32[]{:S(2)}, u32[]{:S(2)}) collective-permute-start(bf16[64,1024]{1,0:T(8,128)(2,1)S(1)} %collective-permute-done.halo_ref), channel_id=1, source_target_pairs={{0,16},{1,17},{2,18},{3,19},{4,20},{5,21},{6,22},{7,23},{8,24},{9,... | collective-permute-start | bytes 393224 | tf_op jit(solution)/shard_map/ppermute | solution.py:204
  33.2 6.6 %copy-start.7 = (f32[8]{0:T(128)S(1)}, f32[8]{0:T(128)}, u32[]{:S(2)}) copy-start(f32[8]{0:T(128)} %param.11) | copy-start | bytes 100
  33.3 6.8 %copy-start.1 = (bf16[81,2048]{1,0:T(8,128)(2,1)S(1)}, bf16[81,2048]{1,0:T(8,128)(2,1)}, u32[]{:S(2)}) copy-start(bf16[81,2048]{1,0:T(8,128)(2,1)} %constant.38.clone.sel2_ref) | copy-start | bytes 995332
  33.3 6.8 %copy-start.2 = (bf16[81,81]{1,0:T(8,128)(2,1)S(1)}, bf16[81,81]{1,0:T(8,128)(2,1)}, u32[]{:S(2)}) copy-start(bf16[81,81]{1,0:T(8,128)(2,1)} %constant.36.clone.mirror_ref) | copy-start | bytes 39370
  34.2 5.8 %copy-start = (bf16[81,2048]{1,0:T(8,128)(2,1)S(1)}, bf16[81,2048]{1,0:T(8,128)(2,1)}, u32[]{:S(2)}) copy-start(bf16[81,2048]{1,0:T(8,128)(2,1)} %constant.37.clone.sel1_ref) | copy-start | bytes 995332
  34.2 12.0 %all-to-all-start.2 = ((bf16[16,36,128]{2,1,0:T(8,128)(2,1)}), bf16[16,36,128]{2,1,0:T(8,128)(2,1)S(1)}, u32[]{:S(2)}, u32[]{:S(2)}) async-start(bf16[16,36,128]{2,1,0:T(8,128)(2,1)} %shard_map.84), calls=%async_computation.2 | async-start | bytes 327680 | tf_op jit(solution)/shard_map/all_to_all | solution.py:240
  40.0 0.7 %copy-start.5 = (f32[8,81]{1,0:T(8,128)S(1)}, f32[8,81]{1,0:T(8,128)}, u32[]{:S(2)}) copy-start(f32[8,81]{1,0:T(8,128)} %cin_ref.1) | copy-start | bytes 7780
  40.0 0.7 %copy-start.6 = (f32[8,81]{1,0:T(8,128)S(1)}, f32[8,81]{1,0:T(8,128)}, u32[]{:S(2)}) copy-start(f32[8,81]{1,0:T(8,128)} %cout_ref.1) | copy-start | bytes 7780

commit v7 on v6

--- a/solution.py
+++ b/solution.py
@@ -115,7 +115,7 @@
     sublane = lax.broadcasted_iota(jnp.int32, (8, 128), 0)
     mine = ((lax.broadcasted_iota(jnp.int32, (36, 128), 1) >> 3) & 1) == y_ref[0]
     for i in range(16):
-        rf_ref[i] = jnp.where(mine, r_ref[i].astype(jnp.float32), r_ref[i ^ 8].astype(jnp.float32))
+        rf_ref[i] = jnp.where(mine, r_ref[i], r_ref[i ^ 8]).astype(jnp.float32)
         for half in range(2):
             rows = [rf_ref[i, pl.ds(half * 12 + d, 8), :] for d in range(0, 24, 8)]
             rows = [shifted(x, s) for s in SHIFTS for x in rows]
@@ -197,9 +197,9 @@
     pairs = []
     for index in range(0, 256, 16):
         if index // 16 % 2:
-            pairs += [(index + t, index + (t ^ 1)) for t in range(16)]
+            pairs += [(index + t, (index ^ 128) + (t ^ 1)) for t in range(16)]
         else:
-            pairs += [(index + t, index + ((t - 1) ^ 1) + 1) for t in range(1, 15)]
+            pairs += [(index + t, (index ^ 128) + ((t - 1) ^ 1) + 1) for t in range(1, 15)]
     halo = lax.ppermute(b, place, pairs)
     swapped = lax.ppermute(halo, place, [(n, n ^ 16) for n in range(256)])
     slot = (lax.axis_index("src") % 2) ^ lax.axis_index("yh")

time: 48.9 us -> 48.9 us (level)
  starting transfers between devices: 28.1 us -> 27.4 us
  waiting for transfers between devices: 13 us -> 13.7 us
    ppermute x1, starting transfers between devices: 4.53 us -> 3.81 us  [per_device(): halo = lax.ppermute(b, place, pairs)]
where the time goes in v7:
time: 48.9 us; the launch traced here: 48.4 us
  starting transfers between devices  27.4 us (56%)
  waiting for transfers between devices  13.7 us (28%)
  Pallas kernels  5.64 us (12%)
  local copies, waits for them, and re-layouts  1.54 us (3%)
    all_to_all x1, starting transfers between devices, per_device(): wide = lax.all_to_all(wide, 'z', 0, 0, tiled=True)  8.19 us
    all_to_all x1, starting transfers between devices, per_device(): b = lax.all_to_all(b, 'src', 0, 0, tiled=True)  6.95 us
    all_to_all x1, starting transfers between devices, per_device(): pieces = lax.all_to_all(pieces, 'src', 0, 0, tiled=True)  5.56 us
    all_to_all x1, waiting for transfers between devices, per_device(): pieces = lax.all_to_all(pieces, 'src', 0, 0, tiled=True)  4.45 us
    ppermute x1, starting transfers between devices, per_device(): halo = lax.ppermute(b, place, pairs)  3.81 us
    ppermute x1, waiting for transfers between devices, per_device(): halo = lax.ppermute(b, place, pairs)  3.4 us
    ppermute x1, starting transfers between devices, per_device(): lax.ppermute(feature_a, ('src', 'z', 'yh'), [(n, n ^ 129) for n in range(...  2.88 us
    pallas_call x1, Pallas kernels, per_device(): pl.pallas_call(consensus_kernel, out_shape=jax.ShapeDtypeStruct((64, 128)...  2.2 us
  transfers between devices with their start and end apart: 6, of which 6 were waited for; matrix products, arithmetic and copies ran while one was open for 1% of the time, Pallas kernels for 4%

profile of v7, /device:TPU:1, one launch (start us, length us, event | category | flops | bytes accessed | tf_op | source)
XLA Modules:
  0.0 48.4 jit_solution(4091250898270292513)
XLA Ops:
  0.0 0.0 copy-start.4
  0.0 0.7 %copy-done.4 = bf16[2,2,1024]{2,1,0:T(2,128)(2,1)S(1)} copy-done((bf16[2,2,1024]{2,1,0:T(2,128)(2,1)S(1)}, bf16[2,2,1024]{2,1,0:T(2,128)(2,1)}, u32[]{:S(2)}) %copy-start.4) | copy-done | bytes 8216
  0.7 0.7 %shard_map.82 = bf16[16,2,2,1024]{3,2,1,0:T(2,128)(2,1)} custom-call(bf16[2,2,1024]{2,1,0:T(2,128)(2,1)S(1)} %copy-done.4), custom_call_target="tpu_custom_call" | custom-call | tf_op jit(solution)/shard_map/pallas_call | solution.py:175
  1.4 0.0 copy-start.3
  1.4 6.9 %all-to-all-start = ((bf16[16,2,2,1024]{3,2,1,0:T(2,128)(2,1)}), bf16[16,2,2,1024]{3,2,1,0:T(2,128)(2,1)S(1)}, u32[]{:S(2)}, u32[]{:S(2)}) async-start(bf16[16,2,2,1024]{3,2,1,0:T(2,128)(2,1)} %shard_map.82), calls=%async_computation | async-start | bytes 262144 | tf_op jit(solution)/shard_map/all_to_all | solution.py:182
  8.3 0.0 copy-done.3
  8.3 2.9 %collective-permute-start.2 = (bf16[1,8,1024]{2,1,0:T(8,128)(2,1)S(1)}, bf16[1,8,1024]{2,1,0:T(8,128)(2,1)S(1)}, u32[]{:S(2)}, u32[]{:S(2)}) collective-permute-start(bf16[1,8,1024]{2,1,0:T(8,128)(2,1)S(1)} %copy-done.3), channel_id=1, source_target_pairs={{0,129},{1,128},{2,131},{3,130},{4,133},{5,132},{6,135},{7,134},{8... | collective-permute-start | bytes 49160 | tf_op jit(solution)/shard_map/ppermute | solution.py:184
  11.2 1.4 %collective-permute-done.2 = bf16[1,8,1024]{2,1,0:T(8,128)(2,1)S(1)} collective-permute-done((bf16[1,8,1024]{2,1,0:T(8,128)(2,1)S(1)}, bf16[1,8,1024]{2,1,0:T(8,128)(2,1)S(1)}, u32[]{:S(2)}, u32[]{:S(2)}) %collective-permute-start.2) | collective-permute-done | bytes 16416 | tf_op jit(solution)/shard_map/ppermute | solution.py:184
  12.6 0.7 %shard_map.83 = bf16[8,2,8,1024]{3,2,1,0:T(8,128)(2,1)} custom-call(bf16[8,1024]{1,0:T(8,128)(2,1)S(1)} %bitcast.9, bf16[8,1024]{1,0:T(8,128)(2,1)S(1)} %bitcast.10, s32[1]{0:T(128)} %bitcast.2.y_ref), custom_call_target="tpu_custom_call" | custom-call | tf_op jit(solution)/shard_map/pallas_call | solution.py:187
  13.3 1.1 %all-to-all-done = bf16[16,2,2,1024]{3,2,1,0:T(2,128)(2,1)S(1)} async-done(((bf16[16,2,2,1024]{3,2,1,0:T(2,128)(2,1)}), bf16[16,2,2,1024]{3,2,1,0:T(2,128)(2,1)S(1)}, u32[]{:S(2)}, u32[]{:S(2)}) %all-to-all-start) | async-done | bytes 131104 | tf_op jit(solution)/shard_map/all_to_all | solution.py:182
  14.4 8.2 %all-to-all-start.1 = ((bf16[8,2,8,1024]{3,2,1,0:T(8,128)(2,1)}), bf16[8,2,8,1024]{3,2,1,0:T(8,128)(2,1)S(1)}, u32[]{:S(2)}, u32[]{:S(2)}) async-start(bf16[8,2,8,1024]{3,2,1,0:T(8,128)(2,1)} %shard_map.83), calls=%async_computation.1 | async-start | bytes 524288 | tf_op jit(solution)/shard_map/all_to_all | solution.py:194
  22.5 0.1 reshape.18.own_ref
  22.6 3.8 %collective-permute-start = (bf16[64,1024]{1,0:T(8,128)(2,1)S(1)}, bf16[64,1024]{1,0:T(8,128)(2,1)S(1)}, u32[]{:S(2)}, u32[]{:S(2)}) collective-permute-start(bf16[64,1024]{1,0:T(8,128)(2,1)S(1)} %reshape.18.own_ref), channel_id=1, source_target_pairs={{1,130},{2,129},{3,132},{4,131},{5,134},{6,133},{7,136},{8,135},{9... | collective-permute-start | bytes 393224 | tf_op jit(solution)/shard_map/ppermute | solution.py:203
  26.4 3.4 %collective-permute-done.halo_ref = bf16[64,1024]{1,0:T(8,128)(2,1)S(1)} collective-permute-done((bf16[64,1024]{1,0:T(8,128)(2,1)S(1)}, bf16[64,1024]{1,0:T(8,128)(2,1)S(1)}, u32[]{:S(2)}, u32[]{:S(2)}) %collective-permute-start) | collective-permute-done | bytes 131104 | tf_op jit(solution)/shard_map/ppermute | solution.py:203
  29.8 0.0 collective-permute-start.1
  29.8 1.3 %collective-permute-done.1.swap_ref = bf16[64,1024]{1,0:T(8,128)(2,1)S(1)} collective-permute-done((bf16[64,1024]{1,0:T(8,128)(2,1)S(1)}, bf16[64,1024]{1,0:T(8,128)(2,1)S(1)}, u32[]{:S(2)}, u32[]{:S(2)}) %collective-permute-start.1) | collective-permute-done | bytes 131104 | tf_op jit(solution)/shard_map/ppermute | solution.py:204
  31.2 2.1 %all-to-all-done.1 = bf16[8,2,8,1024]{3,2,1,0:T(8,128)(2,1)S(1)} async-done(((bf16[8,2,8,1024]{3,2,1,0:T(8,128)(2,1)}), bf16[8,2,8,1024]{3,2,1,0:T(8,128)(2,1)S(1)}, u32[]{:S(2)}, u32[]{:S(2)}) %all-to-all-start.1) | async-done | bytes 262176 | tf_op jit(solution)/shard_map/all_to_all | solution.py:194
  33.2 0.0 copy-start.7
  33.3 0.0 copy-start.1
  33.3 0.0 copy-start.2
  33.3 1.0 %shard_map.84 = bf16[16,36,128]{2,1,0:T(8,128)(2,1)} custom-call(bf16[64,1024]{1,0:T(8,128)(2,1)S(1)} %collective-permute-done.halo_ref, bf16[64,1024]{1,0:T(8,128)(2,1)S(1)} %reshape.18.own_ref, bf16[64,1024]{1,0:T(8,128)(2,1)S(1)} %collective-permute-done.1.swap_ref, bf16[128,1024]{1,0:T(8,128)(2,1)S(1)} %bitcast.8, s32[1]{0:T(128)} %bitcast.4.slot_ref), custom_call_target="tpu_custom_call" | custom-call | flops 67108864 | bytes 1048576 | tf_op jit(solution)/shard_map/pallas_call | solution.py:228
  34.2 0.0 copy-start
  34.2 5.6 %all-to-all-start.2 = ((bf16[16,36,128]{2,1,0:T(8,128)(2,1)}), bf16[16,36,128]{2,1,0:T(8,128)(2,1)S(1)}, u32[]{:S(2)}, u32[]{:S(2)}) async-start(bf16[16,36,128]{2,1,0:T(8,128)(2,1)} %shard_map.84), calls=%async_computation.2 | async-start | bytes 327680 | tf_op jit(solution)/shard_map/all_to_all | solution.py:240
  39.8 0.0 copy-done.7
  39.8 0.1 broadcast_in_dim.11
  39.9 0.1 pad_add_fusion.at_ref
  40.0 0.0 copy-start.5
  40.0 0.0 copy-start.6
  40.0 0.1 broadcast_in_dim.12.bias_ref
  40.1 0.0 copy-done.1
  40.1 0.0 copy-done.2
  40.1 0.0 copy-done
  40.1 0.6 %copy-done.5 = f32[8,81]{1,0:T(8,128)S(1)} copy-done((f32[8,81]{1,0:T(8,128)S(1)}, f32[8,81]{1,0:T(8,128)}, u32[]{:S(2)}) %copy-start.5) | copy-done | bytes 2616
  40.7 0.0 copy-done.6
  40.7 1.1 %shard_map.85 = (bf16[256,256]{1,0:T(8,128)(2,1)S(1)}, bf16[80,256]{1,0:T(8,128)(2,1)S(1)}) custom-call(f32[8,81]{1,0:T(8,128)S(1)} %copy-done.5, f32[8,81]{1,0:T(8,128)S(1)} %copy-done.6, bf16[81,81]{1,0:T(8,128)(2,1)S(1)} %copy-done.2, bf16[81,2048]{1,0:T(8,128)(2,1)S(1)} %copy-done, bf16[81,2048]{1,0:T(8,128)(2,1)S(1)} %copy-done.1, ...), custom_call_target="tpu_custom_call" | custom-call | flops 16777216 | bytes 1048576 | tf_op jit(solution)/shard_map/pallas_call | solution.py:207
  41.8 4.4 %all-to-all-done.2.r_ref = bf16[16,36,128]{2,1,0:T(8,128)(2,1)S(1)} async-done(((bf16[16,36,128]{2,1,0:T(8,128)(2,1)}), bf16[16,36,128]{2,1,0:T(8,128)(2,1)S(1)}, u32[]{:S(2)}, u32[]{:S(2)}) %all-to-all-start.2) | async-done | bytes 147488 | tf_op jit(solution)/shard_map/all_to_all | solution.py:240
  46.2 2.2 %shard_map.86 = f32[64,128]{1,0:T(8,128)} custom-call(bf16[16,36,128]{2,1,0:T(8,128)(2,1)S(1)} %all-to-all-done.2.r_ref, bf16[256,256]{1,0:T(8,128)(2,1)S(1)} %get-tuple-element.7.w1_ref, bf16[80,256]{1,0:T(8,128)(2,1)S(1)} %get-tuple-element.8.w2_ref, s32[1]{0:T(128)} %bitcast.2.y_ref), custom_call_target="tpu_custom_call" | custom-call | flops 268435456 | bytes 1048576 | tf_op jit(solution)/shard_map/pallas_call | solution.py:241
  (1 shorter events, 0.0 us)
Async XLA Ops:
  0.0 0.7 %copy-start.4 = (bf16[2,2,1024]{2,1,0:T(2,128)(2,1)S(1)}, bf16[2,2,1024]{2,1,0:T(2,128)(2,1)}, u32[]{:S(2)}) copy-start(bf16[2,2,1024]{2,1,0:T(2,128)(2,1)} %b_ref.1) | copy-start | bytes 24580
  1.4 7.0 %copy-start.3 = (bf16[1,8,1024]{2,1,0:T(8,128)(2,1)S(1)}, bf16[1,8,1024]{2,1,0:T(8,128)(2,1)}, u32[]{:S(2)}) copy-start(bf16[1,8,1024]{2,1,0:T(8,128)(2,1)} %param.8) | copy-start | bytes 49156
  1.4 13.0 %all-to-all-start = ((bf16[16,2,2,1024]{3,2,1,0:T(2,128)(2,1)}), bf16[16,2,2,1024]{3,2,1,0:T(2,128)(2,1)S(1)}, u32[]{:S(2)}, u32[]{:S(2)}) async-start(bf16[16,2,2,1024]{3,2,1,0:T(2,128)(2,1)} %shard_map.82), calls=%async_computation | async-start | bytes 262144 | tf_op jit(solution)/shard_map/all_to_all | solution.py:182
  8.3 4.3 %collective-permute-start.2 = (bf16[1,8,1024]{2,1,0:T(8,128)(2,1)S(1)}, bf16[1,8,1024]{2,1,0:T(8,128)(2,1)S(1)}, u32[]{:S(2)}, u32[]{:S(2)}) collective-permute-start(bf16[1,8,1024]{2,1,0:T(8,128)(2,1)S(1)} %copy-done.3), channel_id=1, source_target_pairs={{0,129},{1,128},{2,131},{3,130},{4,133},{5,132},{6,135},{7,134},{8... | collective-permute-start | bytes 49160 | tf_op jit(solution)/shard_map/ppermute | solution.py:184
  14.4 18.9 %all-to-all-start.1 = ((bf16[8,2,8,1024]{3,2,1,0:T(8,128)(2,1)}), bf16[8,2,8,1024]{3,2,1,0:T(8,128)(2,1)S(1)}, u32[]{:S(2)}, u32[]{:S(2)}) async-start(bf16[8,2,8,1024]{3,2,1,0:T(8,128)(2,1)} %shard_map.83), calls=%async_computation.1 | async-start | bytes 524288 | tf_op jit(solution)/shard_map/all_to_all | solution.py:194
  22.6 7.2 %collective-permute-start = (bf16[64,1024]{1,0:T(8,128)(2,1)S(1)}, bf16[64,1024]{1,0:T(8,128)(2,1)S(1)}, u32[]{:S(2)}, u32[]{:S(2)}) collective-permute-start(bf16[64,1024]{1,0:T(8,128)(2,1)S(1)} %reshape.18.own_ref), channel_id=1, source_target_pairs={{1,130},{2,129},{3,132},{4,131},{5,134},{6,133},{7,136},{8,135},{9... | collective-permute-start | bytes 393224 | tf_op jit(solution)/shard_map/ppermute | solution.py:203
  29.8 1.3 %collective-permute-start.1 = (bf16[64,1024]{1,0:T(8,128)(2,1)S(1)}, bf16[64,1024]{1,0:T(8,128)(2,1)S(1)}, u32[]{:S(2)}, u32[]{:S(2)}) collective-permute-start(bf16[64,1024]{1,0:T(8,128)(2,1)S(1)} %collective-permute-done.halo_ref), channel_id=1, source_target_pairs={{0,16},{1,17},{2,18},{3,19},{4,20},{5,21},{6,22},{7,23},{8,24},{9,... | collective-permute-start | bytes 393224 | tf_op jit(solution)/shard_map/ppermute | solution.py:204
  33.2 6.6 %copy-start.7 = (f32[8]{0:T(128)S(1)}, f32[8]{0:T(128)}, u32[]{:S(2)}) copy-start(f32[8]{0:T(128)} %param.11) | copy-start | bytes 100
  33.3 6.8 %copy-start.1 = (bf16[81,2048]{1,0:T(8,128)(2,1)S(1)}, bf16[81,2048]{1,0:T(8,128)(2,1)}, u32[]{:S(2)}) copy-start(bf16[81,2048]{1,0:T(8,128)(2,1)} %constant.38.clone.sel2_ref) | copy-start | bytes 995332
  33.3 6.8 %copy-start.2 = (bf16[81,81]{1,0:T(8,128)(2,1)S(1)}, bf16[81,81]{1,0:T(8,128)(2,1)}, u32[]{:S(2)}) copy-start(bf16[81,81]{1,0:T(8,128)(2,1)} %constant.36.clone.mirror_ref) | copy-start | bytes 39370
  34.2 5.8 %copy-start = (bf16[81,2048]{1,0:T(8,128)(2,1)S(1)}, bf16[81,2048]{1,0:T(8,128)(2,1)}, u32[]{:S(2)}) copy-start(bf16[81,2048]{1,0:T(8,128)(2,1)} %constant.37.clone.sel1_ref) | copy-start | bytes 995332
  34.2 12.0 %all-to-all-start.2 = ((bf16[16,36,128]{2,1,0:T(8,128)(2,1)}), bf16[16,36,128]{2,1,0:T(8,128)(2,1)S(1)}, u32[]{:S(2)}, u32[]{:S(2)}) async-start(bf16[16,36,128]{2,1,0:T(8,128)(2,1)} %shard_map.84), calls=%async_computation.2 | async-start | bytes 327680 | tf_op jit(solution)/shard_map/all_to_all | solution.py:240
  40.0 0.7 %copy-start.5 = (f32[8,81]{1,0:T(8,128)S(1)}, f32[8,81]{1,0:T(8,128)}, u32[]{:S(2)}) copy-start(f32[8,81]{1,0:T(8,128)} %cin_ref.1) | copy-start | bytes 7780
  40.0 0.7 %copy-start.6 = (f32[8,81]{1,0:T(8,128)S(1)}, f32[8,81]{1,0:T(8,128)}, u32[]{:S(2)}) copy-start(f32[8,81]{1,0:T(8,128)} %cout_ref.1) | copy-start | bytes 7780
